TPU v7x, 32 devices: a whole 2x2x4 slice. The times are simulated.
32 devices in a mesh: dp: 16 (over z, x, core), tensor: 2 (over y).
Axes of the slice: x: 2, y: 2, z: 4, core: 2. Of those that a mesh axis runs over, the one named last changes fastest.
Arguments:
- tokens: bfloat16 [16, 1024, 2048], P('dp', 'tensor'), may hold values from -6 to 6
- lengths: int32 [16], P('dp'), may hold values from 256 to 1024, as said below
- gain: float32 [2048], replicated, may hold values from 0.1 to 1.9
- w_in: bfloat16 [2048, 2, 4096], P('dp', None, 'tensor'), may hold values from -0.125 to 0.125
- conv_weight: float32 [4, 4096], P(None, 'tensor'), may hold values from -3 to 3
- conv_bias: float32 [4096], P('tensor'), may hold values from -3 to 3
- w_x: bfloat16 [4096, 160], P('tensor'), may hold values from -0.09375 to 0.09375
- w_dt: bfloat16 [128, 4096], P(None, 'tensor'), may hold values from -0.5 to 0.5
- dt_bias: float32 [4096], P('tensor'), may hold values from -5.5 to -2
- a_log: float32 [16, 4096], P(None, 'tensor'), may hold values from -1 to 2.5
- d_skip: float32 [4096], P('tensor'), may hold values from 0.5 to 1.5
- w_out: bfloat16 [4096, 2048], P('tensor', 'dp'), may hold values from -0.1875 to 0.1875
- cotangent: bfloat16 [16, 1024, 2048], P('dp', 'tensor'), may hold values from -6 to 6
Outputs:
- mixed_out: bfloat16 [16, 1024, 2048], P('dp', 'tensor')
- d_tokens: float32 [16, 1024, 2048], P('dp', 'tensor')
- g_gain: float32 [2048], replicated
- g_w_in: float32 [2048, 2, 4096], P('dp', None, 'tensor')
- g_conv_weight: float32 [4, 4096], P(None, 'tensor')
- g_conv_bias: float32 [4096], P('tensor')
- g_w_x: float32 [4096, 160], P('tensor')
- g_w_dt: float32 [128, 4096], P(None, 'tensor')
- g_dt_bias: float32 [4096], P('tensor')
- g_a_log: float32 [16, 4096], P(None, 'tensor')
- g_d_skip: float32 [4096], P('tensor')
- g_w_out: float32 [4096, 2048], P('tensor', 'dp')
Inputs may be any that keep to these rules, and one draw needn't show every extreme that they name: `lengths`: each sequence has at least 256 live slots, and one sequence has 1024; slots at or past a sequence's length are padding.
All inputs are finite; a program needn't handle non-finite values.
Results may differ from a plain program's by a relative error of at most 0.0096.
Values may be sent and summed in bfloat16 or wider, within the bound.
No kernel may reach another device: no remote copies, remote signals or barrier semaphores. Data moves between devices by JAX's collectives and lax.ppermute only.
A program may use at most 512 MiB of HBM per device.

v0:
```python
import jax
import jax.numpy as jnp
from jax import lax
from jax.experimental import pallas as pl
from jax.experimental.pallas import tpu as pltpu
from jax.sharding import PartitionSpec as P


STATE = 16
RANK = 128
CONV = 4
EPS = 1e-05
LIM = 0.3
LOG2E = 1.4426950408889634
LANES = 128
SUB = 8
F32 = jnp.float32
BF = jnp.bfloat16


def work(seconds):
    return pl.CostEstimate(flops=int(seconds * 1e15), transcendentals=0, bytes_accessed=int(seconds * 1e12))


def after(value, *others):
    return lax.optimization_barrier((value,) + others)[0]


def put(ref, v):
    for g in range(ref.shape[0]):
        ref[g] = v[:, g*LANES:(g+1)*LANES]


def take(ref):
    return jnp.concatenate([ref[g] for g in range(ref.shape[0])], axis=1)


def spread_lanes(map_ref, lane_ref):
    high = map_ref[...].astype(BF).astype(F32)
    low = map_ref[...] - high
    spot = lax.broadcasted_iota(jnp.int32, (STATE, LANES), 1)
    ones = jnp.ones((2 * LANES, LANES), BF)

    def octet(i, _):
        base = i * SUB
        picked = [
            jnp.concatenate([jnp.where(spot == base + s, part, 0.0).astype(BF) for part in (high, low)], axis=1)
            for s in range(SUB)
        ]
        start = pl.multiple_of(base * STATE, SUB * STATE)
        lane_ref[pl.ds(start, SUB * STATE), :] = jnp.dot(
            jnp.concatenate(picked, axis=0), ones, preferred_element_type=F32
        )
        return 0

    lax.fori_loop(0, map_ref.shape[1] // SUB, octet, 0, unroll=8)


def rows_of(ref, row):
    return [ref[pl.ds(row + k * SUB, SUB), :] for k in range(2)]


def fold(ref, g):
    total = None
    for r in range(SUB):
        v = ref[g, pl.ds(r, SUB, stride=SUB), :]
        total = v if total is None else total + v
    return total


def fwd_kernel(lowt_ref, wdt_ref, bias_ref, x_ref, bt_ref, ct_ref, alog_ref, y_ref, dt_ref, per_step_ref, per_sum_ref, hs_ref, last_ref, bl_ref, cl_ref,
               h_scr, dt_scr, dtx_scr, p_scr):
    span, width = x_ref.shape
    groups = width // LANES
    tc, cb = pl.program_id(0), pl.program_id(1)

    def sl(g):
        return pl.ds(g * LANES, LANES)

    pre = (
        lax.dot_general(lowt_ref[...], wdt_ref[...], (((0,), (0,)), ((), ())), preferred_element_type=F32)
        + bias_ref[...]
    )
    tail = jnp.exp(-jnp.abs(pre))
    soft = jnp.maximum(pre, 0.0) + jnp.log1p(tail)
    share = LIM / (LIM + soft)
    dt = soft * share
    dt_ref[...] = dt
    slope = jnp.where(pre >= 0.0, 1.0, tail) / (1.0 + tail) * (share * share)
    per_step_ref[...] = slope / jnp.where(dt > 0.0, dt, 1.0)
    per_sum_ref[...] = slope * x_ref[...].astype(F32)
    put(dt_scr, dt)
    put(dtx_scr, dt * x_ref[...].astype(F32))

    @pl.when(tc == 0)
    def _():
        h_scr[cb] = jnp.zeros(h_scr.shape[1:], F32)

    @pl.when(cb == 0)
    def _():
        spread_lanes(bt_ref, bl_ref)
        spread_lanes(ct_ref, cl_ref)

    decay = -jnp.exp(alog_ref[...]) * LOG2E
    rate = [[decay[k * SUB : (k + 1) * SUB, g * LANES : (g + 1) * LANES] for k in range(2)] for g in range(groups)]

    def octet(i, h):
        h = [list(r) for r in h]
        base = pl.multiple_of(i * SUB, SUB)
        for s in range(SUB):
            t = base + s
            row = pl.multiple_of(t * STATE, STATE)
            b, c = rows_of(bl_ref, row), rows_of(cl_ref, row)
            for g in range(groups):
                dtb = dt_scr[g, pl.ds(t, SUB, stride=0), :]
                dxb = dtx_scr[g, pl.ds(t, SUB, stride=0), :]
                q = None
                for k in range(2):
                    hs_ref[pl.ds(row + k * SUB, SUB), sl(g)] = h[g][k]
                    h[g][k] = jnp.exp2(dtb * rate[g][k]) * h[g][k] + b[k] * dxb
                    p = h[g][k] * c[k]
                    q = p if q is None else q + p
                p_scr[g, pl.ds(s * SUB, SUB), :] = q
        for g in range(groups):
            y_ref[pl.ds(base, SUB), sl(g)] = fold(p_scr, g)
        return tuple(tuple(r) for r in h)

    h0 = tuple(tuple(h_scr[cb, pl.ds(k * SUB, SUB), sl(g)] for k in range(2)) for g in range(groups))
    hn = lax.fori_loop(0, span // SUB, octet, h0)
    for g in range(groups):
        for k in range(2):
            h_scr[cb, pl.ds(k * SUB, SUB), sl(g)] = hn[g][k]
            last_ref[pl.ds(k * SUB, SUB), sl(g)] = hn[g][k]


def scan_fwd(low_t, wdt, bias, x, bt, ct, alog, span=LANES, width=1024):
    count, channels = x.shape
    width = min(width, channels)
    nt, nb, rank = count // span, channels // width, wdt.shape[0]
    groups = width // LANES
    tile = pl.BlockSpec((span, width), lambda t, c: (t, c))
    maps = pl.BlockSpec((STATE, span), lambda t, c: (0, t))
    lanes = pl.BlockSpec((span * STATE, LANES), lambda t, c: (t, 0))
    return pl.pallas_call(
        fwd_kernel,
        name="scan_fwd",
        grid=(nt, nb),
        in_specs=[
            pl.BlockSpec((rank, span), lambda t, c: (0, t)),
            pl.BlockSpec((rank, width), lambda t, c: (0, c)),
            pl.BlockSpec((1, width), lambda t, c: (0, c)),
            tile,
            maps,
            maps,
            pl.BlockSpec((STATE, width), lambda t, c: (0, c)),
        ],
        out_specs=[
            tile,
            tile,
            tile,
            tile,
            pl.BlockSpec((span * STATE, width), lambda t, c: (t, c)),
            pl.BlockSpec((STATE, width), lambda t, c: (0, c)),
            lanes,
            lanes,
        ],
        out_shape=[
            jax.ShapeDtypeStruct((count, channels), F32),
            jax.ShapeDtypeStruct((count, channels), F32),
            jax.ShapeDtypeStruct((count, channels), F32),
            jax.ShapeDtypeStruct((count, channels), F32),
            jax.ShapeDtypeStruct((count * STATE, channels), F32),
            jax.ShapeDtypeStruct((STATE, channels), F32),
            jax.ShapeDtypeStruct((count * STATE, LANES), F32),
            jax.ShapeDtypeStruct((count * STATE, LANES), F32),
        ],
        scratch_shapes=[
            pltpu.VMEM((nb, STATE, width), F32),
            pltpu.VMEM((groups, span, LANES), F32),
            pltpu.VMEM((groups, span, LANES), F32),
            pltpu.VMEM((groups, SUB * SUB, LANES), F32),
        ],
        compiler_params=pltpu.CompilerParams(vmem_limit_bytes=58 << 20),
        cost_estimate=work(60e-6),
    )(low_t, wdt, bias.reshape(1, -1), x, bt, ct, alog)


def bwd_kernel(lowt_ref, wdt_ref, x_ref, dm_ref, dt_ref, per_step_ref, per_sum_ref, hs_ref, last_ref, bl_ref, cl_ref, alog_ref, dskip_ref,
               dx_ref, dcp_ref, gwdt_ref, gal_ref, gvec_ref,
               part_scr, g_scr, n_scr, dt_scr, dtx_scr, dm_scr, p1_scr, p2_scr, s1_scr, s2_scr, db_scr, dc_scr):
    span, width = x_ref.shape
    groups = width // LANES
    tc, cb = pl.program_id(0), pl.program_id(1)
    nb = pl.num_programs(1)

    def sl(g):
        return pl.ds(g * LANES, LANES)

    put(dt_scr, dt_ref[...])
    put(dtx_scr, dt_ref[...] * x_ref[...].astype(F32))
    put(dm_scr, dm_ref[...])

    @pl.when(tc == 0)
    def _():
        g_scr[cb] = jnp.zeros(g_scr.shape[1:], F32)
        n_scr[cb] = last_ref[...]
        gal_ref[cb] = jnp.zeros(gal_ref.shape[1:], F32)
        gvec_ref[cb] = jnp.zeros(gvec_ref.shape[1:], F32)
        gwdt_ref[cb] = jnp.zeros(gwdt_ref.shape[1:], F32)

    @pl.when(cb == 0)
    def _():
        db_scr[...] = jnp.zeros_like(db_scr)
        dc_scr[...] = jnp.zeros_like(dc_scr)
        part_scr[...] = jnp.zeros_like(part_scr)

    decay = -jnp.exp(alog_ref[...]) * LOG2E
    rate = [[decay[k * SUB : (k + 1) * SUB, g * LANES : (g + 1) * LANES] for k in range(2)] for g in range(groups)]

    def octet(j, carry):
        ag, ga, hn = [[list(r) for r in c] for c in carry]
        base = pl.multiple_of((span // SUB - 1 - j) * SUB, SUB)
        for s in reversed(range(SUB)):
            t = base + s
            row = pl.multiple_of(t * STATE, STATE)
            b, c = rows_of(bl_ref, row), rows_of(cl_ref, row)
            db = [db_scr[pl.ds(row + k * SUB, SUB), :] for k in range(2)]
            dc = [dc_scr[pl.ds(row + k * SUB, SUB), :] for k in range(2)]
            for g in range(groups):
                dtb = dt_scr[g, pl.ds(t, SUB, stride=0), :]
                dxb = dtx_scr[g, pl.ds(t, SUB, stride=0), :]
                dmb = dm_scr[g, pl.ds(t, SUB, stride=0), :]
                q1 = q2 = None
                for k in range(2):
                    hp = hs_ref[pl.ds(row + k * SUB, SUB), sl(g)]
                    da = dtb * rate[g][k]
                    adj = c[k] * dmb + ag[g][k]
                    dc[k] = dc[k] + dmb * hn[g][k]
                    db[k] = db[k] + adj * dxb
                    nag = jnp.exp2(da) * adj
                    q = (nag * hp) * da
                    ga[g][k] = ga[g][k] + q
                    gb = adj * b[k]
                    q1 = gb if q1 is None else q1 + gb
                    q2 = q if q2 is None else q2 + q
                    ag[g][k] = nag
                    hn[g][k] = hp
                p1_scr[g, pl.ds(s * SUB, SUB), :] = q1
                p2_scr[g, pl.ds(s * SUB, SUB), :] = q2
            for k in range(2):
                db_scr[pl.ds(row + k * SUB, SUB), :] = db[k]
                dc_scr[pl.ds(row + k * SUB, SUB), :] = dc[k]
        for g in range(groups):
            s1_scr[g, pl.ds(base, SUB), :] = fold(p1_scr, g)
            s2_scr[g, pl.ds(base, SUB), :] = fold(p2_scr, g)
        return tuple(tuple(tuple(r) for r in c) for c in (ag, ga, hn))

    def held(ref):
        return tuple(tuple(ref[cb, pl.ds(k * SUB, SUB), sl(g)] for k in range(2)) for g in range(groups))

    zero = jnp.zeros((SUB, LANES), F32)
    ga0 = tuple(tuple(zero for _ in range(2)) for _ in range(groups))
    ag, ga, hn = lax.fori_loop(0, span // SUB, octet, (held(g_scr), ga0, held(n_scr)))
    for g in range(groups):
        for k in range(2):
            g_scr[cb, pl.ds(k * SUB, SUB), sl(g)] = ag[g][k]
            n_scr[cb, pl.ds(k * SUB, SUB), sl(g)] = hn[g][k]
            gal_ref[cb, pl.ds(k * SUB, SUB), sl(g)] += ga[g][k] * (1.0 / LOG2E)
    dt = dt_ref[...]
    x = x_ref[...].astype(F32)
    dm = dm_ref[...]
    s1 = take(s1_scr)
    s2 = take(s2_scr) * (1.0 / LOG2E)
    dx_ref[...] = dm * dskip_ref[...] + dt * s1
    d_pre = s2 * per_step_ref[...] + s1 * per_sum_ref[...]
    gvec_ref[cb, 0:1, :] += jnp.sum(d_pre, axis=0, keepdims=True)
    gvec_ref[cb, 1:2, :] += jnp.sum(dm * x, axis=0, keepdims=True)
    dlow = d_pre.astype(BF)
    gwdt_ref[cb] += jnp.dot(lowt_ref[...], dlow, preferred_element_type=F32)
    part_scr[...] += lax.dot_general(wdt_ref[...], dlow, (((1,), (1,)), ((), ())), preferred_element_type=F32)

    @pl.when(cb == nb - 1)
    def _():
        rank = part_scr.shape[0]
        dcp_ref[0:rank, :] = part_scr[...].astype(dcp_ref.dtype)
        ones = jnp.ones((STATE, LANES), BF)
        state = lax.broadcasted_iota(jnp.int32, (STATE, span * STATE), 0)
        spot = lax.broadcasted_iota(jnp.int32, (STATE, span * STATE), 1)
        row = lax.broadcasted_iota(jnp.int32, (span * STATE, span), 0)
        slot = lax.broadcasted_iota(jnp.int32, (span * STATE, span), 1)
        pick = jnp.where(row // STATE == slot, 1.0, 0.0).astype(BF)
        for n, ref in enumerate((db_scr, dc_scr)):
            total = lax.dot_general(ones, ref[...].astype(BF), (((1,), (1,)), ((), ())), preferred_element_type=F32)
            kept = jnp.where(spot % STATE == state, total, 0.0).astype(BF)
            at = rank + n * STATE
            dcp_ref[at : at + STATE, :] = jnp.dot(kept, pick, preferred_element_type=F32).astype(dcp_ref.dtype)


def scan_bwd(low_t, wdt, x, dm, dt, per_step, per_sum, hs, last, bl, cl, alog, dskip, span=LANES, width=1024):
    count, channels = x.shape
    width = min(width, channels)
    nt, nb, rank = count // span, channels // width, wdt.shape[0]
    groups = width // LANES
    tile = pl.BlockSpec((span, width), lambda t, c: (nt - 1 - t, c))
    lanes = pl.BlockSpec((span * STATE, LANES), lambda t, c: (nt - 1 - t, 0))
    return pl.pallas_call(
        bwd_kernel,
        name="scan_bwd",
        grid=(nt, nb),
        in_specs=[
            pl.BlockSpec((rank, span), lambda t, c: (0, nt - 1 - t)),
            pl.BlockSpec((rank, width), lambda t, c: (0, c)),
            tile,
            tile,
            tile,
            tile,
            tile,
            pl.BlockSpec((span * STATE, width), lambda t, c: (nt - 1 - t, c)),
            pl.BlockSpec((STATE, width), lambda t, c: (0, c)),
            lanes,
            lanes,
            pl.BlockSpec((STATE, width), lambda t, c: (0, c)),
            pl.BlockSpec((1, width), lambda t, c: (0, c)),
        ],
        out_specs=[
            tile,
            pl.BlockSpec((rank + 2 * STATE, span), lambda t, c: (0, nt - 1 - t)),
            pl.BlockSpec((nb, rank, width), lambda t, c: (0, 0, 0)),
            pl.BlockSpec((nb, STATE, width), lambda t, c: (0, 0, 0)),
            pl.BlockSpec((nb, 2, width), lambda t, c: (0, 0, 0)),
        ],
        out_shape=[
            jax.ShapeDtypeStruct((count, channels), F32),
            jax.ShapeDtypeStruct((rank + 2 * STATE, count), BF),
            jax.ShapeDtypeStruct((nb, rank, width), F32),
            jax.ShapeDtypeStruct((nb, STATE, width), F32),
            jax.ShapeDtypeStruct((nb, 2, width), F32),
        ],
        scratch_shapes=[
            pltpu.VMEM((rank, span), F32),
            *[pltpu.VMEM((nb, STATE, width), F32)] * 2,
            *[pltpu.VMEM((groups, span, LANES), F32)] * 3,
            *[pltpu.VMEM((groups, SUB * SUB, LANES), F32)] * 2,
            *[pltpu.VMEM((groups, span, LANES), F32)] * 2,
            *[pltpu.VMEM((span * STATE, LANES), F32)] * 2,
        ],
        compiler_params=pltpu.CompilerParams(vmem_limit_bytes=58 << 20),
        cost_estimate=work(110e-6),
    )(low_t, wdt, x, dm, dt, per_step, per_sum, hs, last, bl, cl, alog, dskip.reshape(1, -1))


def taps_at(pad_ref, g, row, rows):
    return [pad_ref[g, pl.ds(row + SUB - (CONV - 1) + j, rows), :] for j in range(CONV)]


def pre_of(taps, cw_ref, cb_ref, lanes):
    pre = cb_ref[:, lanes]
    for j in range(CONV):
        pre = pre + cw_ref[j : j + 1, lanes] * taps[j]
    return pre


def conv_kernel(inner_ref, wxt_ref, cw_ref, cb_ref, conv_ref, cpl_ref, pad_ref, sum_ref):
    count, width = inner_ref.shape
    rows = 128

    @pl.when(pl.program_id(0) == 0)
    def _():
        sum_ref[...] = jnp.zeros_like(sum_ref)

    for g in range(width // LANES):
        lanes = slice(g * LANES, (g + 1) * LANES)
        pad_ref[g, 0:SUB, :] = jnp.zeros((SUB, LANES), F32)
        pad_ref[g, SUB:, :] = inner_ref[:, lanes]

        def chunk(i, _, g=g, lanes=lanes):
            row = pl.multiple_of(i * rows, rows)
            pre = pre_of(taps_at(pad_ref, g, row, rows), cw_ref, cb_ref, lanes)
            conv_ref[pl.ds(row, rows), lanes] = (pre * jax.nn.sigmoid(pre)).astype(BF)
            return 0

        lax.fori_loop(0, count // rows, chunk, 0)
    sum_ref[...] += lax.dot_general(
        wxt_ref[...], conv_ref[...], (((1,), (1,)), ((), ())), preferred_element_type=F32
    )

    @pl.when(pl.program_id(0) == pl.num_programs(0) - 1)
    def _():
        cpl_ref[...] = sum_ref[...].astype(cpl_ref.dtype)


def conv_forward(inner, wxt, cw, cb, dtype, width=256):
    count, channels = inner.shape
    width = min(width, channels)
    cols = wxt.shape[0]
    return pl.pallas_call(
        conv_kernel,
        name="conv_forward",
        grid=(channels // width,),
        in_specs=[
            pl.BlockSpec((count, width), lambda c: (0, c)),
            pl.BlockSpec((cols, width), lambda c: (0, c)),
            pl.BlockSpec((CONV, width), lambda c: (0, c)),
            pl.BlockSpec((1, width), lambda c: (0, c)),
        ],
        out_specs=[
            pl.BlockSpec((count, width), lambda c: (0, c)),
            pl.BlockSpec((cols, count), lambda c: (0, 0)),
        ],
        out_shape=[
            jax.ShapeDtypeStruct((count, channels), BF),
            jax.ShapeDtypeStruct((cols, count), dtype),
        ],
        scratch_shapes=[pltpu.VMEM((width // LANES, count + SUB, LANES), F32), pltpu.VMEM((cols, count), F32)],
        compiler_params=pltpu.CompilerParams(vmem_limit_bytes=40 << 20),
        cost_estimate=work(12e-6),
    )(inner, wxt, cw, cb.reshape(1, -1))


def conv_back_kernel(inner_ref, dx_ref, dcp_ref, dcpt_ref, wxt_ref, cw_ref, cb_ref, din_ref, gsum_ref, gwx_ref,
                     pad_ref, dpre_ref, low_ref, back_ref):
    count, width = inner_ref.shape
    rows = 64
    back_ref[...] = jnp.dot(dcp_ref[...], wxt_ref[...], preferred_element_type=F32)
    gsum_ref[CONV + 1 :, :] = jnp.zeros((SUB - CONV - 1, width), F32)
    for g in range(width // LANES):
        lanes = slice(g * LANES, (g + 1) * LANES)
        pad_ref[g, 0:SUB, :] = jnp.zeros((SUB, LANES), F32)
        pad_ref[g, SUB:, :] = inner_ref[:, lanes]
        dpre_ref[g, count:, :] = jnp.zeros((SUB, LANES), F32)

        def chunk(i, sums, g=g, lanes=lanes):
            row = pl.multiple_of(i * rows, rows)
            taps = taps_at(pad_ref, g, row, rows)
            pre = pre_of(taps, cw_ref, cb_ref, lanes)
            gate = jax.nn.sigmoid(pre)
            conv = pre * gate
            low_ref[pl.ds(row, rows), lanes] = conv.astype(BF)
            d_pre = (dx_ref[pl.ds(row, rows), lanes] + back_ref[pl.ds(row, rows), lanes]) * (gate + conv - conv * gate)
            dpre_ref[g, pl.ds(row, rows), :] = d_pre
            new = [d_pre * t for t in taps] + [d_pre]
            return tuple(
                s + sum(n[k * SUB : (k + 1) * SUB] for k in range(rows // SUB)) for s, n in zip(sums, new)
            )

        zero = jnp.zeros((SUB, LANES), F32)
        sums = lax.fori_loop(0, count // rows, chunk, (zero,) * (CONV + 1))
        for j in range(CONV + 1):
            gsum_ref[j : j + 1, lanes] = jnp.sum(sums[j], axis=0, keepdims=True)

        def shift(i, _, g=g, lanes=lanes):
            row = pl.multiple_of(i * rows, rows)
            total = None
            for j in range(CONV):
                v = cw_ref[j : j + 1, lanes] * dpre_ref[g, pl.ds(row + CONV - 1 - j, rows), :]
                total = v if total is None else total + v
            din_ref[pl.ds(row, rows), lanes] = total.astype(BF)
            return 0

        lax.fori_loop(0, count // rows, shift, 0)
    gwx_ref[...] = jnp.dot(dcpt_ref[...], low_ref[...], preferred_element_type=F32)


def conv_back(inner, dx, dcpt, wxt, cw, cb, width=256):
    count, channels = inner.shape
    width = min(width, channels)
    cols = wxt.shape[0]
    return pl.pallas_call(
        conv_back_kernel,
        name="conv_back",
        grid=(channels // width,),
        in_specs=[
            pl.BlockSpec((count, width), lambda c: (0, c)),
            pl.BlockSpec((count, width), lambda c: (0, c)),
            pl.BlockSpec((count, cols), lambda c: (0, 0)),
            pl.BlockSpec((cols, count), lambda c: (0, 0)),
            pl.BlockSpec((cols, width), lambda c: (0, c)),
            pl.BlockSpec((CONV, width), lambda c: (0, c)),
            pl.BlockSpec((1, width), lambda c: (0, c)),
        ],
        out_specs=[
            pl.BlockSpec((count, width), lambda c: (0, c)),
            pl.BlockSpec((SUB, width), lambda c: (0, c)),
            pl.BlockSpec((cols, width), lambda c: (0, c)),
        ],
        out_shape=[
            jax.ShapeDtypeStruct((count, channels), BF),
            jax.ShapeDtypeStruct((SUB, channels), F32),
            jax.ShapeDtypeStruct((cols, channels), F32),
        ],
        scratch_shapes=[
            pltpu.VMEM((width // LANES, count + SUB, LANES), F32),
            pltpu.VMEM((width // LANES, count + SUB, LANES), F32),
            pltpu.VMEM((count, width), BF),
            pltpu.VMEM((count, width), F32),
        ],
        compiler_params=pltpu.CompilerParams(vmem_limit_bytes=40 << 20),
        cost_estimate=work(15e-6),
    )(inner, dx, dcpt.T, dcpt, wxt, cw, cb.reshape(1, -1))


def dual_kernel(which_ref, a_ref, b_ref, wa_ref, wb_ref, norm_ref, out_ref, sum_ref):
    del which_ref
    nt = (((1,), (1,)), ((), ()))
    out = lax.dot_general(a_ref[...], wa_ref[...], nt, preferred_element_type=F32)
    out = out + lax.dot_general(b_ref[...], wb_ref[...], nt, preferred_element_type=F32)
    out_ref[...] = out.astype(out_ref.dtype)
    sum_ref[...] = jnp.sum(norm_ref[...].astype(F32) * out, axis=0, keepdims=True)


def dual_product(which, rows, a, b, wa, wb, norm, dtype, tile=512):
    depth, count = a.shape[1], wa.shape[0]
    left = pl.BlockSpec((rows, depth), lambda n, w: (w[0], 0))
    right = pl.BlockSpec((tile, depth), lambda n, w: (n, 0))
    return pl.pallas_call(
        dual_kernel,
        name="dual_product",
        grid_spec=pltpu.PrefetchScalarGridSpec(
            num_scalar_prefetch=1,
            grid=(count // tile,),
            in_specs=[left, left, right, right, pl.BlockSpec((rows, tile), lambda n, w: (w[0], n))],
            out_specs=[
                pl.BlockSpec((rows, tile), lambda n, w: (0, n)),
                pl.BlockSpec((1, tile), lambda n, w: (0, n)),
            ],
        ),
        out_shape=[jax.ShapeDtypeStruct((rows, count), dtype), jax.ShapeDtypeStruct((1, count), F32)],
        compiler_params=pltpu.CompilerParams(vmem_limit_bytes=40 << 20),
        cost_estimate=work(15e-6),
    )(which.reshape(1).astype(jnp.int32), a, b, wa, wb, norm)


def swap(value):
    return lax.ppermute(value, "tensor", [(0, 1), (1, 0)])


def ordered(own, other):
    first = lax.axis_index("tensor") == 0
    return jnp.concatenate([jnp.where(first, own, other), jnp.where(first, other, own)], axis=0)


def gather_rows(own):
    if lax.axis_size("tensor") != 2:
        return lax.all_gather(own, "tensor", axis=0, tiled=True)
    return ordered(own, swap(own))


def total_tensor(part):
    if lax.axis_size("tensor") != 2:
        return lax.psum(part.astype(F32), "tensor")
    return part.astype(F32) + swap(part).astype(F32)


def dp_spot():
    index = lax.axis_index("dp")
    return index // 4, (index // 2) % 2, index % 2


def over_core(v):
    return lax.ppermute(v, "dp", [(i, i ^ 1) for i in range(16)])


def over_x(v):
    return lax.ppermute(v, "dp", [(i, i ^ 2) for i in range(16)])


def over_near(v):
    return lax.ppermute(v, "dp", [(i, i ^ 4) for i in range(16)])


def over_far(v):
    return lax.ppermute(v, "dp", [(i, i ^ 8) for i in range(16)])


def over_z(v, shift):
    return lax.ppermute(v, "dp", [(i, (i + 4 * shift) % 16) for i in range(16)])


def part_of(v, which, count):
    size = v.shape[0] // count
    return lax.dynamic_slice_in_dim(v, which * size, size, 0)


def pick(v, which, axis):
    return lax.dynamic_index_in_dim(v, which, axis, keepdims=False)


def add_low(*terms):
    return sum(t.astype(F32) for t in terms).astype(BF)


def paired(own, other, place):
    first = place == 0
    return jnp.concatenate([jnp.where(first, own, other), jnp.where(first, other, own)], axis=0)


def mm(a, b):
    return jnp.dot(a, b, preferred_element_type=F32)


def mm_nt(a, b):
    return lax.dot_general(a, b, (((1,), (1,)), ((), ())), preferred_element_type=F32)


def mm_tn(a, b):
    return lax.dot_general(a, b, (((0,), (0,)), ((), ())), preferred_element_type=F32)


def rows_out(residual, branch, length, first_row):
    live = first_row + jnp.arange(residual.shape[0], dtype=jnp.int32) < length
    return (residual + jnp.where(live[:, None], branch, 0.0)).astype(BF)


def rows_back(cotangent, residual, scale, gain, d_normed):
    weighted = d_normed * gain
    return (
        cotangent[0].astype(F32)
        + scale * weighted
        - residual * (scale * scale * scale) * jnp.mean(residual * weighted, axis=1, keepdims=True)
    )


def body(
    tokens,
    lengths,
    gain,
    w_in,
    conv_weight,
    conv_bias,
    w_x,
    w_dt,
    dt_bias,
    a_log,
    d_skip,
    w_out,
    cotangent,
):
    rows_here = tokens.shape[1]
    width = conv_bias.shape[0]
    total_rows = rows_here * lax.axis_size("tensor")
    paired_tensor = lax.axis_size("tensor") == 2
    grouped_dp = lax.axis_size("dp") == 16
    length = lengths[0]
    side = lax.axis_index("tensor")
    residual = tokens[0].astype(F32)
    scale = lax.rsqrt(jnp.mean(residual * residual, axis=1, keepdims=True) + EPS)
    normed = gather_rows((residual * scale * gain).astype(BF))
    cot_own = after(cotangent[0], normed)
    cot_other = swap(cot_own) if paired_tensor else lax.all_gather(cot_own, "tensor", axis=0, tiled=True)
    w_inner = lax.all_gather(w_in[:, 0], "dp", axis=0, tiled=True)
    w_gate = lax.all_gather(after(w_in, scale)[:, 1], "dp", axis=0, tiled=True)
    out_full = lax.all_gather(after(w_out, scale).T, "dp", axis=0, tiled=True)
    w_x_t = w_x.T

    inner = mm(normed, w_inner)
    conv_low, part = conv_forward(inner, w_x_t, conv_weight, conv_bias, BF)
    cot_own, cot_other, part_kept = lax.optimization_barrier((cot_own, cot_other, part))
    cot_rows = ordered(cot_own, cot_other) if paired_tensor else cot_other
    live_all = jnp.arange(total_rows, dtype=jnp.int32) < length
    d_branch = jnp.where(live_all[:, None], cot_rows, jnp.zeros_like(cot_rows))
    if paired_tensor:
        coupled = part_kept.astype(F32) + after(swap(part), d_branch).astype(F32)
    else:
        coupled = total_tensor(part)
    low_t = coupled[:RANK].astype(BF)
    scanned, step_size, per_step, per_sum, states, last, input_lanes, output_lanes = scan_fwd(
        low_t, w_dt, dt_bias, conv_low, coupled[RANK : RANK + STATE], coupled[RANK + STATE :], a_log
    )
    w_gate, scanned = lax.optimization_barrier((w_gate, scanned))
    gate_in = mm(normed, w_gate)
    sig = jax.nn.sigmoid(gate_in)
    opened = gate_in * sig
    mixed = scanned + d_skip * conv_low.astype(F32)
    gated = (mixed * opened).astype(BF)

    def spread(grad):
        return lax.psum_scatter(grad, "dp", scatter_dimension=0, tiled=True)

    part_out = mm_tn(d_branch, gated).astype(BF)
    g_w_out = spread(part_out)
    out_full = after(out_full, part_out)
    d_gated = mm(d_branch, out_full)
    d_mixed = d_gated * opened
    d_gate = (d_gated * mixed * (sig * (1.0 + gate_in * (1.0 - sig)))).astype(BF)
    part_gate = mm_tn(normed, d_gate).astype(BF)
    g_w_gate = spread(part_gate)

    def halves(v, which):
        return lax.dynamic_slice_in_dim(v, which * rows_here, rows_here, 0)

    d_mixed = after(d_mixed, part_gate)
    if not paired_tensor:
        branch = lax.psum_scatter(mm_nt(gated, out_full), "tensor", scatter_dimension=0, tiled=True)

    d_scan, d_part, g_w_dt, g_a_log, g_vec = scan_bwd(
        low_t,
        w_dt,
        conv_low,
        d_mixed,
        step_size,
        per_step,
        per_sum,
        states,
        last,
        input_lanes,
        output_lanes,
        a_log,
        d_skip,
    )

    def joined(blocks):
        return jnp.swapaxes(blocks, 0, 1).reshape(blocks.shape[1], width)

    def packed(pieces):
        held = sum(p.shape[0] for p in pieces)
        padded = -(-held // 64) * 64
        return jnp.concatenate([p.astype(BF) for p in pieces] + [jnp.zeros((padded - held, width), BF)], axis=0)

    if paired_tensor:
        branch_sent = mm_nt(after(halves(gated, 1 - side), d_part), out_full).astype(BF)
        d_coupled = (d_part.astype(F32) + after(swap(d_part), branch_sent).astype(F32)).astype(BF)
        branch_got = swap(after(branch_sent, d_coupled))
    else:
        d_coupled = total_tensor(d_part).astype(BF)
    d_inner, g_conv, g_w_x = conv_back(inner, d_scan, d_coupled, w_x_t, conv_weight, conv_bias)
    smalls = [joined(g_w_dt), joined(g_a_log), joined(g_vec), g_w_x, g_conv]
    if not grouped_dp or not paired_tensor:
        smalls = lax.psum(packed(smalls), "dp").astype(F32)
        g_w_inner = spread(mm_tn(normed, d_inner).astype(BF)).astype(F32)
        d_normed = lax.psum_scatter(
            mm_nt(d_inner, w_inner) + mm_nt(d_gate, w_gate), "tensor", scatter_dimension=0, tiled=True
        )
        g_gain = lax.psum(jnp.sum(residual * scale * d_normed, axis=0), ("dp", "tensor"))
        if paired_tensor:
            branch = mm_nt(halves(gated, side), out_full) + branch_got.astype(F32)
        d_rows = rows_back(cotangent, residual, scale, gain, d_normed)
        mixed_out = rows_out(residual, branch, length, side * rows_here)
    else:
        z, x, c = dp_spot()
        own, cut = w_in.shape[0], (7 * width) // 16

        pack = packed(smalls)
        core_got = over_core(part_of(pack, 1 - c, 2))
        part_b = mm_tn(after(normed, pack), d_inner[:, cut:]).astype(BF)
        half = add_low(part_of(pack, c, 2), after(core_got, part_b))
        x_got = over_x(part_of(half, 1 - x, 2))
        chips = after(part_b, half).reshape(8, 2, own, width - cut)
        chip_sent = pick(chips, 1 - c, 1)
        chip_got = over_core(chip_sent)
        part_a = mm_tn(after(normed, chip_sent), d_inner[:, :cut]).astype(BF)
        g_a = spread(part_a)
        quarter = add_low(part_of(half, x, 2), after(x_got, part_a))
        near_got = over_near(quarter)
        chip = add_low(pick(chips, c, 1), after(chip_got, quarter)).reshape(4, 2, own, width - cut)
        row_sent = pick(chip, 1 - x, 1)
        row_got = over_x(row_sent)
        sent, gain_sent = dual_product(
            1 - side, rows_here, after(d_inner, row_sent), d_gate, w_inner, w_gate, normed, BF
        )
        normed_got = swap(sent)
        pair = add_low(quarter, after(near_got, sent))
        far_got = over_far(pair)
        kept, gain_kept = dual_product(side, rows_here, after(d_inner, pair), d_gate, w_inner, w_gate, normed, F32)
        g_gain = gain_sent + gain_kept
        gain_got = over_core(g_gain)
        row = add_low(pick(chip, x, 1), after(row_got, kept))
        column_sent = [pick(row, (z + k) % 4, 0) for k in (1, 2, 3)]
        column_got = [over_z(column_sent[k - 1], k) for k in (1, 2, 3)]
        whole = add_low(pair, *lax.optimization_barrier((far_got,) + tuple(column_sent))[:1])
        x_got = over_x(whole)
        g_gain = g_gain + after(gain_got, whole)
        gain_got = over_x(g_gain)
        branch = mm_nt(after(halves(gated, side), g_gain), out_full) + branch_got.astype(F32)
        mixed_out = rows_out(residual, branch, length, side * rows_here)
        half = paired(whole, after(x_got, mixed_out), x)
        core_got = over_core(half)
        g_gain = g_gain + after(gain_got, mixed_out)
        gain_got = over_near(g_gain)
        smalls = paired(half, after(core_got, g_gain), c).astype(F32)
        g_gain = g_gain + after(gain_got, smalls)
        gain_got = over_far(g_gain)
        d_normed = kept + after(normed_got, g_gain).astype(F32)
        d_rows = rows_back(cotangent, residual, scale, gain, d_normed)
        g_gain = g_gain + after(gain_got, d_rows)
        gain_got = swap(g_gain)
        g_b = sum(
            (v.astype(F32) for v in lax.optimization_barrier(tuple(column_got) + (d_rows, g_gain))[:3]),
            pick(row, z, 0).astype(F32),
        )
        g_gain = (g_gain + after(gain_got, g_b))[0] / gain
        g_w_inner = jnp.concatenate([after(g_a, g_b).astype(F32), g_b], axis=1)

    g_w_dt = smalls[:RANK]
    at = RANK + STATE
    g_a_log = smalls[RANK:at]
    g_dt_bias, g_d_skip = smalls[at], smalls[at + 1]
    at += 2
    g_w_x = smalls[at : at + RANK + 2 * STATE].T
    at += RANK + 2 * STATE
    g_conv_weight = smalls[at : at + CONV]
    g_conv_bias = smalls[at + CONV]
    g_w_gate, g_w_out = lax.optimization_barrier((g_w_gate, g_w_out, d_rows))[:2]
    g_w_in = jnp.stack([g_w_inner, g_w_gate.astype(F32)], axis=1)
    return (
        mixed_out[None],
        d_rows[None],
        g_gain,
        g_w_in,
        g_conv_weight,
        g_conv_bias,
        g_w_x,
        g_w_dt,
        g_dt_bias,
        g_a_log,
        g_d_skip,
        g_w_out.T.astype(F32),
    )


def solution(mesh):
    placed = (
        P("dp", "tensor", None),
        P("dp"),
        P(),
        P("dp", None, "tensor"),
        P(None, "tensor"),
        P("tensor"),
        P("tensor", None),
        P(None, "tensor"),
        P("tensor"),
        P(None, "tensor"),
        P("tensor"),
        P("tensor", "dp"),
        P("dp", "tensor", None),
    )
    return jax.shard_map(
        body,
        mesh=mesh,
        in_specs=placed,
        out_specs=(
            P("dp", "tensor", None),
            P("dp", "tensor", None),
            P(),
            P("dp", None, "tensor"),
            P(None, "tensor"),
            P("tensor"),
            P("tensor", None),
            P(None, "tensor"),
            P("tensor"),
            P(None, "tensor"),
            P("tensor"),
            P("tensor", "dp"),
        ),
        check_vma=False,
    )
```

profile of v0, /device:TPU:0, one launch (start us, length us, event | category | flops | bytes accessed | tf_op | source)
XLA Modules:
  0.0 762.7 jit_solution(10798541737376069903)
XLA Ops:
  7.3 2.5 copy.41
  9.8 2.1 fusion.2
  13.8 1.9 fusion.4
  15.6 3.0 collective-permute-start
  19.4 45.2 %collective-permute-done = bf16[512,2048]{1,0:T(8,128)(2,1)} collective-permute-done((bf16[512,2048]{1,0:T(8,128)(2,1)}, bf16[512,2048]{1,0:T(8,128)(2,1)}, u32[]{:S(2)}, u32[]{:S(2)}) %collective-permute-start) | collective-permute-done | bytes 2097184 | tf_op jit(solution)/shard_map/ppermute | solution.py:534
  64.6 3.1 broadcast_select_fusion.3
  67.7 2.6 pad_maximum_fusion.norm_ref
  71.1 1.8 collective-permute-start.1
  72.9 14.9 %all-gather.10.cloned.1.call-done = bf16[2048,1,2048]{2,0,1:T(8,128)(2,1)} async-done(((bf16[128,1,2048]{2,0,1:T(8,128)(2,1)}), bf16[2048,1,2048]{2,0,1:T(8,128)(2,1)}) %all-gather.10.cloned.1.call-update) | async-done | bytes 8388624 | tf_op jit(solution)/shard_map/all_gather | solution.py:650
  87.8 12.5 %fusion.15.inner_ref = f32[1024,2048]{1,0:T(8,128)S(1)} fusion(bf16[2048,1,2048]{2,0,1:T(8,128)(2,1)} %all-gather.10.cloned.1.call-done, bf16[512,2048]{1,0:T(8,128)(2,1)} %copy-done.20, bf16[512,2048]{1,0:T(8,128)(2,1)} %copy-done.18), kind=kOutput, calls=%fused_computation.73 | convolution fusion | flops 8598323200 | bytes 20971520 | tf_op jit(solution)/shard_map/dot_general | solution.py:598
  100.3 9.3 %conv_forward.1 = (bf16[1024,2048]{1,0:T(8,128)(2,1)S(1)}, bf16[160,1024]{1,0:T(8,128)(2,1)S(1)}) custom-call(f32[1024,2048]{1,0:T(8,128)S(1)} %fusion.15.inner_ref, bf16[160,2048]{1,0:T(8,128)(2,1)S(1)} %bitcast.92, f32[4,2048]{1,0:T(4,128)S(1)} %copy-done.4, f32[1,2048]{1,0:T(1,128)S(1)} %bitcast.94), custom_call_target="tpu_custom_call" | custom-call | flops 12000000000 | bytes 12000000 | tf_op jit(solution)/shard_map/conv_forward/pallas_call | solution.py:396
  109.7 1.5 collective-permute-start.2
  111.3 8.5 %collective-permute-done.1 = bf16[512,2048]{1,0:T(8,128)(2,1)} collective-permute-done((bf16[512,2048]{1,0:T(8,128)(2,1)S(1)}, bf16[512,2048]{1,0:T(8,128)(2,1)}, u32[]{:S(2)}, u32[]{:S(2)}) %collective-permute-start.1) | collective-permute-done | bytes 2097184 | tf_op jit(solution)/shard_map/ppermute | solution.py:534
  119.8 1.9 broadcast_select_fusion.1
  121.6 7.1 maximum_select_fusion
  130.2 73.8 %scan_fwd.1 = (f32[1024,2048]{1,0:T(8,128)}, f32[1024,2048]{1,0:T(8,128)}, f32[1024,2048]{1,0:T(8,128)}, f32[1024,2048]{1,0:T(8,128)}, f32[16384,2048]{1,0:T(8,1...) custom-call(bf16[128,1024]{1,0:T(8,128)(2,1)} %slice.74.lowt_ref, bf16[128,2048]{1,0:T(8,128)(2,1)} %wdt_ref.3, ...), custom_call_target="tpu_custom_call" | custom-call | flops 60000002048 | bytes 60000000 | tf_op jit(solution)/shard_map/scan_fwd/pallas_call | solution.py:144
  204.1 18.2 %multiply_convert_fusion.1 = (bf16[1024,2048]{1,0:T(8,128)(2,1)S(1)}, f32[1024,2048]{1,0:T(8,128)}) fusion(f32[1024,2048]{1,0:T(8,128)} %get-tuple-element.83, bf16[1024,2048]{1,0:T(8,128)(2,1)} %copy-done.12, f32[2048]{0:T(1024)S(1)} %copy-done.40, bf16[2048,2048]{1,0:T(8,128)(2,1)} %bitcast.114, bf16[512,2048]{1,0:T(8,128)(2,1)} %copy-done.20, ...), kind=kOutput, calls=%fused_computation.6 | convolution fusion | flops 8617197568 | bytes 37756928 | tf_op jit(solution)/shard_map/dot_general | solution.py:598
  222.3 2.0 copy-done.23
  224.3 13.6 %convolution_convert_fusion.2 = bf16[2048,2048]{1,0:T(8,128)(2,1)} fusion(bf16[1024,2048]{1,0:T(8,128)(2,1)} %maximum_select_fusion, bf16[1024,2048]{1,0:T(8,128)(2,1)S(1)} %get-tuple-element.182), kind=kOutput, calls=%fused_computation.12 | convolution fusion | flops 8594128896 | bytes 16777216 | tf_op jit(solution)/shard_map/dot_general | solution.py:606
  237.8 4.1 all-gather.6.cloned.1.call-done
  241.9 22.5 %multiply_convert_fusion = (bf16[1024,2048]{1,0:T(8,128)(2,1)}, f32[1024,2048]{1,0:T(8,128)}) fusion(f32[1024,2048]{1,0:T(8,128)} %get-tuple-element.183, f32[1024,2048]{1,0:T(8,128)} %get-tuple-element.83, bf16[1024,2048]{1,0:T(8,128)(2,1)} %copy-done.12, f32[2048]{0:T(1024)S(1)} %copy-done.40, bf16[1024,2048]{1,0:T(8,128)(2,1)} %maximum_select_fusion, ...), kind=kOutput, calls=%fused_computation.5 | convolution fusion | flops 8621391872 | bytes 46145536 | tf_op jit(solution)/shard_map/dot_general | solution.py:598
  264.5 13.7 %convolution_convert_fusion.1 = bf16[2048,2048]{1,0:T(8,128)(2,1)} fusion(bf16[1024,2048]{1,0:T(8,128)(2,1)} %get-tuple-element.160.b_ref, bf16[512,2048]{1,0:T(8,128)(2,1)} %copy-done.20, bf16[512,2048]{1,0:T(8,128)(2,1)S(1)} %copy-done.19), kind=kOutput, calls=%fused_computation.11 | convolution fusion | flops 8602517504 | bytes 16777216 | tf_op jit(solution)/shard_map/dot_general | solution.py:606
  278.1 111.3 %scan_bwd.1 = (f32[1024,2048]{1,0:T(8,128)}, bf16[160,1024]{1,0:T(8,128)(2,1)}, f32[2,128,1024]{2,1,0:T(8,128)}, f32[2,16,1024]{2,1,0:T(8,128)}, f32[2,2,1024]{2,1,0:T(2,128)}) custom-call(bf16[128,1024]{1,0:T(8,128)(2,1)} %slice.74.lowt_ref, bf16[128,2048]{1,0:T(8,128)(2,1)} %wdt_ref.3, bf16[1024,2048]{1,0:T(8,128)(2,1)} %copy-done.12, ...), custom_call_target="tpu_custom_call" | custom-call | flops 109999996928 | bytes 110000000 | tf_op jit(solution)/shard_map/scan_bwd/pallas_call | solution.py:306
  389.5 1.6 collective-permute-start.3
  391.0 1.9 constant_dynamic-slice_fusion.2
  393.5 6.1 convolution_convert_fusion.4
  400.7 21.1 %conv_back.1 = (bf16[1024,2048]{1,0:T(8,128)(2,1)S(1)}, f32[8,2048]{1,0:T(8,128)S(1)}, f32[160,2048]{1,0:T(8,128)S(1)}) custom-call(f32[1024,2048]{1,0:T(8,128)} %copy-done.10, f32[1024,2048]{1,0:T(8,128)} %get-tuple-element.95.dx_ref, bf16[1024,160]{1,0:T(8,128)(2,1)S(1)} %copy.34.dcp_ref, bf16[160,1024]{1,0:T(8,128)(2,1)S(1)} %add_convert_fusion.4.dcpt_ref, ...), custom_call_target="tpu_custom_call" | custom-call | flops 15000000512 | bytes 15000000 | tf_op jit(solution)/shard_map/conv_back/pallas_call | solution.py:468
  421.9 2.0 copy-done.8
  424.0 1.1 concatenate.20
  425.5 8.2 %convolution_convert_fusion = bf16[2048,1152]{1,0:T(8,128)(2,1)S(1)} fusion(bf16[1024,2048]{1,0:T(8,128)(2,1)} %pad_maximum_fusion.norm_ref, bf16[1024,2048]{1,0:T(8,128)(2,1)} %copy-done.8), kind=kOutput, calls=%fused_computation.10 | convolution fusion | flops 4834197504 | bytes 11272192 | tf_op jit(solution)/shard_map/dot_general | solution.py:606
  434.0 2.2 copy-done.21
  436.1 1.6 dynamic-slice_bitcast_fusion
  438.5 7.5 convolution_convert_fusion.3
  446.9 1.6 collective-permute-start.6
  448.5 1.6 collective-permute-start.11
  450.1 6.8 collective-permute-done.6
  457.1 3.3 fusion.1
  460.6 1.5 collective-permute-start.10
  462.5 12.3 %dual_product.2 = (bf16[512,2048]{1,0:T(8,128)(2,1)S(1)}, f32[1,2048]{1,0:T(1,128)S(1)}) custom-call(s32[1]{0:T(128)} %bitcast.10.which_ref, bf16[1024,2048]{1,0:T(8,128)(2,1)S(1)} %copy-done.9, bf16[1024,2048]{1,0:T(8,128)(2,1)S(1)} %copy-done.11, bf16[2048,2048]{1,0:T(8,128)(2,1)} %bitcast.112, bf16[2048,2048]{1,0:T(8,128)(2,1)} %bitcast.115, ...), custom_call_target="tpu_custom_call" | custom-call | flops 15000000512 | bytes 15000000 | tf_op jit(solution)/shard_map/dual_product/pallas_call | solution.py:515
  474.9 1.7 collective-permute-start.9
  476.6 1.5 collective-permute-start.12
  478.0 12.1 %dual_product.3 = (f32[512,2048]{1,0:T(8,128)S(1)}, f32[1,2048]{1,0:T(1,128)S(1)}) custom-call(s32[1]{0:T(128)} %bitcast.23.which_ref, bf16[1024,2048]{1,0:T(8,128)(2,1)S(1)} %copy-done.9, bf16[1024,2048]{1,0:T(8,128)(2,1)S(1)} %copy-done.11, bf16[2048,2048]{1,0:T(8,128)(2,1)} %bitcast.113, bf16[2048,2048]{1,0:T(8,128)(2,1)} %bitcast.116, ...), custom_call_target="tpu_custom_call" | custom-call | flops 15000000512 | bytes 15000000 | tf_op jit(solution)/shard_map/dual_product/pallas_call | solution.py:515
  490.3 7.6 collective-permute-done.10
  498.2 1.0 dynamic-slice_bitcast_fusion.2
  499.2 3.3 collective-permute-start.15
  502.6 9.7 %fusion.5 = bf16[512,2048]{1,0:T(8,128)(2,1)} fusion(bf16[512,2048]{1,0:T(8,128)(2,1)S(1)} %collective-permute-done.11, bf16[1,512,2048]{2,1,0:T(8,128)(2,1)S(1)} %copy-done.14, pred[512]{0:T(512)(128)(4,1)S(1)} %add_compare_fusion, bf16[512,2048]{1,0:T(8,128)(2,1)S(1)} %copy-done.28, bf16[2048,2048]{0,1:T(8,128)(2,1)} %all-gather.6.cloned.1.call-done), kind=kOutput, calls=%fused_computation.18 | convolution fusion | flops 4301258752 | bytes 16777728 | tf_op jit(solution)/shard_map/dot_general | solution.py:602
  514.0 0.9 collective-permute-start.19
  514.9 2.2 collective-permute-start.20
  517.6 2.5 collective-permute-start.21
  520.3 1.6 broadcast_select_fusion.5
  522.2 16.4 %collective-permute-done.14 = f32[1,2048]{1,0:T(1,128)S(1)} collective-permute-done((f32[1,2048]{1,0:T(1,128)S(1)}, f32[1,2048]{1,0:T(1,128)S(1)}, u32[]{:S(2)}, u32[]{:S(2)}) %collective-permute-start.14) | collective-permute-done | bytes 8224 | tf_op jit(solution)/shard_map/ppermute | solution.py:568
  538.7 3.8 collective-permute-start.17
  542.5 2.6 fusion.8
  545.1 1.2 slice_bitcast_fusion
  546.3 4.7 fusion.7
  551.6 1.1 slice.64
  554.0 1.5 collective-permute-start.18
  555.7 2.0 collective-permute-done.18
  558.3 1.0 convert_element_type.239
  559.5 83.5 %reduce-scatter.6.cloned.1.call-done = bf16[128,2048]{1,0:T(8,128)(2,1)} async-done(((bf16[2048,2048]{1,0:T(8,128)(2,1)}), bf16[128,2048]{1,0:T(8,128)(2,1)}) %reduce-scatter.6.cloned.1.call-update) | async-done | bytes 524304 | tf_op jit(solution)/shard_map/reduce_scatter | solution.py:677
  642.9 107.0 %reduce-scatter.8.cloned.1.call-done = bf16[128,2048]{1,0:T(8,128)(2,1)} async-done(((bf16[2048,2048]{1,0:T(8,128)(2,1)}), bf16[128,2048]{1,0:T(8,128)(2,1)}) %reduce-scatter.8.cloned.1.call-update) | async-done | bytes 524304 | tf_op jit(solution)/shard_map/reduce_scatter | solution.py:677
  749.9 1.1 bitcast_convert_fusion
  751.3 2.9 copy.39
  754.4 1.3 copy.40
  (160 shorter events, 15.2 us)
Async XLA Ops:
  7.2 5.3 copy-start.25
  7.2 6.6 copy-start.13
  7.2 6.5 copy-start.32
  7.2 80.6 %all-gather.10.cloned.1.call-start = ((), (), s32[]{:S(2)}) async-start(), calls=%async_computation.8 | async-start | bytes 8912896 | tf_op jit(solution)/shard_map/all_gather | solution.py:650
  9.8 194.3 %all-gather.8.cloned.1.call-start = ((), (), s32[]{:S(2)}) async-start(), calls=%async_computation.7 | async-start | bytes 8912896 | tf_op jit(solution)/shard_map/all_gather | solution.py:651
  12.5 52.1 %copy-start.35 = (f32[512]{0:T(512)}, f32[512]{0:T(512)S(1)}, u32[]{:S(2)}) copy-start(f32[512]{0:T(512)S(1)} %get-tuple-element.181) | copy-start | bytes 6148
  13.7 228.3 %all-gather.6.cloned.1.call-start = ((), (), s32[]{:S(2)}) async-start(), calls=%async_computation.3 | async-start | bytes 8912896 | tf_op jit(solution)/shard_map/all_gather | solution.py:652
  15.6 48.9 %collective-permute-start = (bf16[512,2048]{1,0:T(8,128)(2,1)}, bf16[512,2048]{1,0:T(8,128)(2,1)}, u32[]{:S(2)}, u32[]{:S(2)}) collective-permute-start(bf16[512,2048]{1,0:T(8,128)(2,1)} %fusion.4), channel_id=1, source_target_pairs={{0,1},{1,0},{2,3},{3,2},{4,5},{5,4},{6,7},{7,6},{8,9},{9,8},{10,11... | collective-permute-start | bytes 6291464 | tf_op jit(solution)/shard_map/ppermute | solution.py:534
  18.6 539.7 %reduce-scatter.4.cloned.1.call-start = ((), (), s32[]{:S(2)}) async-start(), calls=%async_computation.4 | async-start | bytes 3899392 | tf_op jit(solution)/shard_map/reduce_scatter | solution.py:677
  67.6 2.7 copy-start.18
  67.6 3.4 copy-start.20
  67.7 3.4 copy-start.16
  71.1 29.2 %copy-start.2 = (bf16[2048,160]{0,1:T(8,128)(2,1)S(1)}, bf16[2048,160]{0,1:T(8,128)(2,1)}, u32[]{:S(2)}) copy-start(bf16[2048,160]{0,1:T(8,128)(2,1)} %param.19) | copy-start | bytes 1966084
  71.1 29.3 %copy-start.4 = (f32[4,2048]{1,0:T(4,128)S(1)}, f32[4,2048]{1,0:T(4,128)}, u32[]{:S(2)}) copy-start(f32[4,2048]{1,0:T(4,128)} %cw_ref.3) | copy-start | bytes 98308
  71.1 29.3 %copy-start.6 = (f32[2048]{0:T(1024)S(1)}, f32[2048]{0:T(1024)}, u32[]{:S(2)}) copy-start(f32[2048]{0:T(1024)} %param.18) | copy-start | bytes 24580
  71.1 48.7 %collective-permute-start.1 = (bf16[512,2048]{1,0:T(8,128)(2,1)S(1)}, bf16[512,2048]{1,0:T(8,128)(2,1)}, u32[]{:S(2)}, u32[]{:S(2)}) collective-permute-start(bf16[512,2048]{1,0:T(8,128)(2,1)S(1)} %bitcast.98), channel_id=1, source_target_pairs={{0,1},{1,0},{2,3},{3,2},{4,5},{5,4},{6,7},{7,6},{8,9},{9,8},{10,11... | collective-permute-start | bytes 6291464 | tf_op jit(solution)/shard_map/ppermute | solution.py:534
  100.3 9.4 %copy-start.10 = (f32[1024,2048]{1,0:T(8,128)}, f32[1024,2048]{1,0:T(8,128)S(1)}, u32[]{:S(2)}) copy-start(f32[1024,2048]{1,0:T(8,128)S(1)} %fusion.15.inner_ref) | copy-start | bytes 25165828
  109.7 11.9 %copy-start.12 = (bf16[1024,2048]{1,0:T(8,128)(2,1)}, bf16[1024,2048]{1,0:T(8,128)(2,1)S(1)}, u32[]{:S(2)}) copy-start(bf16[1024,2048]{1,0:T(8,128)(2,1)S(1)} %get-tuple-element.81.x_ref) | copy-start | bytes 12582916
  109.7 19.0 %collective-permute-start.2 = (bf16[160,1024]{1,0:T(8,128)(2,1)S(1)}, bf16[160,1024]{1,0:T(8,128)(2,1)S(1)}, u32[]{:S(2)}, u32[]{:S(2)}) collective-permute-start(bf16[160,1024]{1,0:T(8,128)(2,1)S(1)} %get-tuple-element.77), channel_id=1, source_target_pairs={{0,1},{1,0},{2,3},{3,2},{4,5},{5,4},{6,7},{7,6},{8,9},{9,8},{10,11... | collective-permute-start | bytes 983048 | tf_op jit(solution)/shard_map/ppermute | solution.py:534
  130.2 73.8 %copy-start.19 = (bf16[512,2048]{1,0:T(8,128)(2,1)S(1)}, bf16[512,2048]{1,0:T(8,128)(2,1)}, u32[]{:S(2)}) copy-start(bf16[512,2048]{1,0:T(8,128)(2,1)} %copy-done.18) | copy-start | bytes 6291460
  130.2 73.8 %copy-start.40 = (f32[2048]{0:T(1024)S(1)}, f32[2048]{0:T(1024)}, u32[]{:S(2)}) copy-start(f32[2048]{0:T(1024)} %param.23) | copy-start | bytes 24580
  222.3 2.0 copy-start.23
  278.1 112.9 %copy-start.24 = (bf16[1024,2048]{1,0:T(8,128)(2,1)S(1)}, bf16[1024,2048]{1,0:T(8,128)(2,1)}, u32[]{:S(2)}) copy-start(bf16[1024,2048]{1,0:T(8,128)(2,1)} %copy-done.23) | copy-start | bytes 12582916
  389.5 4.0 copy-start.39
  389.5 10.4 %collective-permute-start.3 = (bf16[160,1024]{1,0:T(8,128)(2,1)}, bf16[160,1024]{1,0:T(8,128)(2,1)S(1)}, u32[]{:S(2)}, u32[]{:S(2)}) collective-permute-start(bf16[160,1024]{1,0:T(8,128)(2,1)} %get-tuple-element.96), channel_id=1, source_target_pairs={{0,1},{1,0},{2,3},{3,2},{4,5},{5,4},{6,7},{7,6},{8,9},{9,8},{10,11... | collective-permute-start | bytes 983048 | tf_op jit(solution)/shard_map/ppermute | solution.py:534
  393.5 6.2 copy-start.29
  393.5 6.3 copy-start.34
  393.5 6.3 copy-start.37
  393.5 6.3 copy-start.31
  421.9 2.0 copy-start.8
  425.1 8.6 %collective-permute-start.4 = (bf16[160,2048]{1,0:T(8,128)(2,1)S(1)}, bf16[160,2048]{1,0:T(8,128)(2,1)S(1)}, u32[]{:S(2)}, u32[]{:S(2)}) collective-permute-start(bf16[160,2048]{1,0:T(8,128)(2,1)S(1)} %constant_dynamic-slice_fusion.1), channel_id=1, source_target_pairs={{0,2},{2,0},{4,6},{6,4},{8,10},{10,8},{12,14},{14,12},{16,18},{18,... | collective-permute-start | bytes 1966088 | tf_op jit(solution)/shard_map/ppermute | solution.py:560
  433.7 2.4 copy-start.21
  433.7 4.7 copy-start.22
  446.0 196.9 %reduce-scatter.6.cloned.1.call-start = ((), (), s32[]{:S(2)}) async-start(), calls=%async_computation.5 | async-start | bytes 8912896 | tf_op jit(solution)/shard_map/reduce_scatter | solution.py:677
  446.6 303.3 %reduce-scatter.8.cloned.1.call-start = ((), (), s32[]{:S(2)}) async-start(), calls=%async_computation.6 | async-start | bytes 8912896 | tf_op jit(solution)/shard_map/reduce_scatter | solution.py:677
  446.7 10.5 %collective-permute-start.5 = (bf16[8,128,1152]{2,1,0:T(8,128)(2,1)}, bf16[8,128,1152]{2,1,0:T(8,128)(2,1)}, u32[]{:S(2)}, u32[]{:S(2)}) collective-permute-start(bf16[8,128,1152]{2,1,0:T(8,128)(2,1)} %dynamic-slice_bitcast_fusion), channel_id=1, source_target_pairs={{0,2},{2,0},{4,6},{6,4},{8,10},{10,8},{12,14},{14,12},{16,18},{18,... | collective-permute-start | bytes 7077896 | tf_op jit(solution)/shard_map/ppermute | solution.py:560
  446.9 10.0 %collective-permute-start.6 = (bf16[80,2048]{1,0:T(8,128)(2,1)S(1)}, bf16[80,2048]{1,0:T(8,128)(2,1)S(1)}, u32[]{:S(2)}, u32[]{:S(2)}) collective-permute-start(bf16[80,2048]{1,0:T(8,128)(2,1)S(1)} %constant_dynamic-slice_fusion), channel_id=1, source_target_pairs={{0,4},{2,6},{4,0},{6,2},{8,12},{10,14},{12,8},{14,10},{16,20},{18,... | collective-permute-start | bytes 983048 | tf_op jit(solution)/shard_map/ppermute | solution.py:564
  448.5 54.1 %collective-permute-start.11 = (bf16[512,2048]{1,0:T(8,128)(2,1)}, bf16[512,2048]{1,0:T(8,128)(2,1)S(1)}, u32[]{:S(2)}, u32[]{:S(2)}) collective-permute-start(bf16[512,2048]{1,0:T(8,128)(2,1)} %convolution_convert_fusion.4), channel_id=1, source_target_pairs={{0,1},{1,0},{2,3},{3,2},{4,5},{5,4},{6,7},{7,6},{8,9},{9,8},{10,11... | collective-permute-start | bytes 6291464 | tf_op jit(solution)/shard_map/ppermute | solution.py:534
  457.0 5.1 copy-start.9
  457.0 5.5 copy-start.11
  457.1 17.7 %collective-permute-start.7 = (bf16[80,2048]{1,0:T(8,128)(2,1)S(1)}, bf16[80,2048]{1,0:T(8,128)(2,1)S(1)}, u32[]{:S(2)}, u32[]{:S(2)}) collective-permute-start(bf16[80,2048]{1,0:T(8,128)(2,1)S(1)} %add_convert_fusion.3), channel_id=1, source_target_pairs={{0,8},{2,10},{4,12},{6,14},{8,0},{10,2},{12,4},{14,6},{16,24},{18,... | collective-permute-start | bytes 983048 | tf_op jit(solution)/shard_map/ppermute | solution.py:568
  460.6 37.3 %collective-permute-start.10 = (bf16[4,128,1152]{2,1,0:T(8,128)(2,1)S(1)}, bf16[4,128,1152]{2,1,0:T(8,128)(2,1)S(1)}, u32[]{:S(2)}, u32[]{:S(2)}) collective-permute-start(bf16[4,128,1152]{2,1,0:T(8,128)(2,1)S(1)} %dynamic-slice_bitcast_fusion.1), channel_id=1, source_target_pairs={{0,4},{2,6},{4,0},{6,2},{8,12},{10,14},{12,8},{14,10},{16,20},{18,... | collective-permute-start | bytes 3538952 | tf_op jit(solution)/shard_map/ppermute | solution.py:564
  474.9 24.3 %collective-permute-start.9 = (bf16[80,2048]{1,0:T(8,128)(2,1)S(1)}, bf16[80,2048]{1,0:T(8,128)(2,1)S(1)}, u32[]{:S(2)}, u32[]{:S(2)}) collective-permute-start(bf16[80,2048]{1,0:T(8,128)(2,1)S(1)} %add_convert_fusion.2), channel_id=1, source_target_pairs={{0,16},{2,18},{4,20},{6,22},{8,24},{10,26},{12,28},{14,30},{16,0},... | collective-permute-start | bytes 983048 | tf_op jit(solution)/shard_map/ppermute | solution.py:572
  476.6 65.9 %collective-permute-start.12 = (bf16[512,2048]{1,0:T(8,128)(2,1)S(1)}, bf16[512,2048]{1,0:T(8,128)(2,1)}, u32[]{:S(2)}, u32[]{:S(2)}) collective-permute-start(bf16[512,2048]{1,0:T(8,128)(2,1)S(1)} %get-tuple-element.113), channel_id=1, source_target_pairs={{0,1},{1,0},{2,3},{3,2},{4,5},{5,4},{6,7},{7,6},{8,9},{9,8},{10,11... | collective-permute-start | bytes 6291464 | tf_op jit(solution)/shard_map/ppermute | solution.py:534
  490.2 22.1 %copy-start = (f32[512,2048]{1,0:T(8,128)}, f32[512,2048]{1,0:T(8,128)S(1)}, u32[]{:S(2)}) copy-start(f32[512,2048]{1,0:T(8,128)S(1)} %get-tuple-element.117) | copy-start | bytes 12582916
  490.2 12.4 %copy-start.14 = (bf16[1,512,2048]{2,1,0:T(8,128)(2,1)S(1)}, bf16[1,512,2048]{2,1,0:T(8,128)(2,1)}, u32[]{:S(2)}) copy-start(bf16[1,512,2048]{2,1,0:T(8,128)(2,1)} %param.13) | copy-start | bytes 6291460
  490.2 12.4 %copy-start.28 = (bf16[512,2048]{1,0:T(8,128)(2,1)S(1)}, bf16[512,2048]{1,0:T(8,128)(2,1)}, u32[]{:S(2)}) copy-start(bf16[512,2048]{1,0:T(8,128)(2,1)} %get-tuple-element.121) | copy-start | bytes 6291460
  490.2 12.3 %collective-permute-start.8 = (f32[1,2048]{1,0:T(1,128)S(1)}, f32[1,2048]{1,0:T(1,128)S(1)}, u32[]{:S(2)}, u32[]{:S(2)}) collective-permute-start(f32[1,2048]{1,0:T(1,128)S(1)} %add.205), channel_id=1, source_target_pairs={{0,2},{2,0},{4,6},{6,4},{8,10},{10,8},{12,14},{14,12},{16,18},{18,... | collective-permute-start | bytes 24584 | tf_op jit(solution)/shard_map/ppermute | solution.py:560
  499.2 13.1 %collective-permute-start.15 = (bf16[80,2048]{1,0:T(8,128)(2,1)S(1)}, bf16[80,2048]{1,0:T(8,128)(2,1)S(1)}, u32[]{:S(2)}, u32[]{:S(2)}) collective-permute-start(bf16[80,2048]{1,0:T(8,128)(2,1)S(1)} %add_convert_fusion.1), channel_id=1, source_target_pairs={{0,4},{2,6},{4,0},{6,2},{8,12},{10,14},{12,8},{14,10},{16,20},{18,... | collective-permute-start | bytes 983048 | tf_op jit(solution)/shard_map/ppermute | solution.py:564
  512.4 30.1 %copy-start.33 = (f32[2048]{0:T(1024)S(1)}, f32[2048]{0:T(1024)}, u32[]{:S(2)}) copy-start(f32[2048]{0:T(1024)} %param.15) | copy-start | bytes 24580
  514.0 6.2 collective-permute-start.16
  514.0 3.7 collective-permute-start.13
  514.0 28.5 %copy-start.1 = (f32[512,2048]{1,0:T(8,128)S(1)}, f32[512,2048]{1,0:T(8,128)}, u32[]{:S(2)}) copy-start(f32[512,2048]{1,0:T(8,128)} %copy-done) | copy-start | bytes 12582916
  514.0 28.5 %copy-start.15 = (bf16[1,512,2048]{2,1,0:T(8,128)(2,1)S(1)}, bf16[1,512,2048]{2,1,0:T(8,128)(2,1)}, u32[]{:S(2)}) copy-start(bf16[1,512,2048]{2,1,0:T(8,128)(2,1)} %param.13) | copy-start | bytes 6291460
  514.0 41.5 %collective-permute-start.19 = (bf16[128,1152]{1,0:T(8,128)(2,1)}, bf16[128,1152]{1,0:T(8,128)(2,1)S(1)}, u32[]{:S(2)}, u32[]{:S(2)}) collective-permute-start(bf16[128,1152]{1,0:T(8,128)(2,1)} %get-tuple-element.175), channel_id=1, source_target_pairs={{0,8},{2,10},{4,12},{6,14},{8,16},{10,18},{12,20},{14,22},{16,24},... | collective-permute-start | bytes 884744 | tf_op jit(solution)/shard_map/ppermute | solution.py:576
  514.9 40.6 %collective-permute-start.20 = (bf16[128,1152]{1,0:T(8,128)(2,1)}, bf16[128,1152]{1,0:T(8,128)(2,1)S(1)}, u32[]{:S(2)}, u32[]{:S(2)}) collective-permute-start(bf16[128,1152]{1,0:T(8,128)(2,1)} %get-tuple-element.174), channel_id=1, source_target_pairs={{0,16},{2,18},{4,20},{6,22},{8,24},{10,26},{12,28},{14,30},{16,0},... | collective-permute-start | bytes 884744 | tf_op jit(solution)/shard_map/ppermute | solution.py:576
  517.6 37.9 %collective-permute-start.21 = (bf16[128,1152]{1,0:T(8,128)(2,1)}, bf16[128,1152]{1,0:T(8,128)(2,1)S(1)}, u32[]{:S(2)}, u32[]{:S(2)}) collective-permute-start(bf16[128,1152]{1,0:T(8,128)(2,1)} %get-tuple-element.173), channel_id=1, source_target_pairs={{0,24},{2,26},{4,28},{6,30},{8,0},{10,2},{12,4},{14,6},{16,8},{18,... | collective-permute-start | bytes 884744 | tf_op jit(solution)/shard_map/ppermute | solution.py:576
  520.2 18.4 %collective-permute-start.14 = (f32[1,2048]{1,0:T(1,128)S(1)}, f32[1,2048]{1,0:T(1,128)S(1)}, u32[]{:S(2)}, u32[]{:S(2)}) collective-permute-start(f32[1,2048]{1,0:T(1,128)S(1)} %add.221), channel_id=1, source_target_pairs={{0,8},{2,10},{4,12},{6,14},{8,0},{10,2},{12,4},{14,6},{16,24},{18,... | collective-permute-start | bytes 24584 | tf_op jit(solution)/shard_map/ppermute | solution.py:568
  538.6 7.7 %copy-start.17 = (bf16[1,512,2048]{2,1,0:T(8,128)(2,1)S(1)}, bf16[1,512,2048]{2,1,0:T(8,128)(2,1)}, u32[]{:S(2)}) copy-start(bf16[1,512,2048]{2,1,0:T(8,128)(2,1)} %param.25) | copy-start | bytes 6291460
  538.6 7.7 %copy-start.36 = (f32[512]{0:T(512)S(1)}, f32[512]{0:T(512)}, u32[]{:S(2)}) copy-start(f32[512]{0:T(512)} %copy-done.35) | copy-start | bytes 6148
  538.6 7.7 %copy-start.38 = (f32[512]{0:T(512)S(1)}, f32[512]{0:T(512)}, u32[]{:S(2)}) copy-start(f32[512]{0:T(512)} %get-tuple-element.180) | copy-start | bytes 6148
  538.7 15.3 %collective-permute-start.17 = (f32[1,2048]{1,0:T(1,128)S(1)}, f32[1,2048]{1,0:T(1,128)S(1)}, u32[]{:S(2)}, u32[]{:S(2)}) collective-permute-start(f32[1,2048]{1,0:T(1,128)S(1)} %add.222), channel_id=1, source_target_pairs={{0,16},{2,18},{4,20},{6,22},{8,24},{10,26},{12,28},{14,30},{16,0},... | collective-permute-start | bytes 24584 | tf_op jit(solution)/shard_map/ppermute | solution.py:572
  554.0 3.7 collective-permute-start.18
  751.1 3.2 copy-start.30
  (5 other events, 5.6 us)
Sparse Core Ops, SparseCore 0:
  10.8 77.0 all-gather.9
  90.5 72.8 all-gather.7
  165.6 76.2 all-gather.5
  446.1 91.6 reduce-scatter.3
  541.8 101.0 reduce-scatter.5
  646.8 103.0 reduce-scatter.7
where the time goes:
time: 772 us; the launch traced here: 763 us
  waiting for transfers between devices  297 us (38%)
  Pallas kernels  240 us (31%)
  matrix products  112 us (15%)
  other arithmetic  37.1 us (5%)
  starting transfers between devices  31.2 us (4%)
  local copies, waits for them, and re-layouts  29.4 us (4%)
  between operations  15.8 us (2%)
    reduce_scatter x3, waiting for transfers between devices, spread(): return lax.psum_scatter(grad, 'dp', scatter_dimension=0, tiled=True)  190 us
    pallas_call x1, Pallas kernels, scan_bwd(): pl.pallas_call(bwd_kernel, name='scan_bwd', grid=(nt, nb), in_specs=[pl.B...  111 us
    pallas_call x1, Pallas kernels, scan_fwd(): pl.pallas_call(fwd_kernel, name='scan_fwd', grid=(nt, nb), in_specs=[pl.B...  73.8 us
    ppermute x7, waiting for transfers between devices, swap(): return lax.ppermute(value, 'tensor', [(0, 1), (1, 0)])  55.7 us
    dot_general x3, matrix products, mm(): return jnp.dot(a, b, preferred_element_type=F32)  53.2 us
    dot_general x4, matrix products, mm_tn(): lax.dot_general(a, b, (((0,), (0,)), ((), ())), preferred_element_type=F32)  42.9 us
    pallas_call x2, Pallas kernels, dual_product(): pl.pallas_call(dual_kernel, name='dual_product', grid_spec=pltpu.Prefetch...  24.4 us
    pallas_call x1, Pallas kernels, conv_back(): pl.pallas_call(conv_back_kernel, name='conv_back', grid=(channels // widt...  21.1 us
  transfers between devices with their start and end apart: 28, of which 11 were waited for; matrix products, arithmetic and copies ran while one was open for 15% of the time, Pallas kernels for 14%

commit v1 on v0

--- a/solution.py
+++ b/solution.py
@@ -68,7 +68,7 @@
     return total
 
 
-def fwd_kernel(lowt_ref, wdt_ref, bias_ref, x_ref, bt_ref, ct_ref, alog_ref, y_ref, dt_ref, per_step_ref, per_sum_ref, hs_ref, last_ref, bl_ref, cl_ref,
+def fwd_kernel(lowt_ref, wdt_ref, bias_ref, x_ref, bt_ref, ct_ref, alog_ref, y_ref, dt_ref, slope_ref, hs_ref, last_ref, bl_ref, cl_ref,
                h_scr, dt_scr, dtx_scr, p_scr):
     span, width = x_ref.shape
     groups = width // LANES
@@ -86,9 +86,7 @@
     share = LIM / (LIM + soft)
     dt = soft * share
     dt_ref[...] = dt
-    slope = jnp.where(pre >= 0.0, 1.0, tail) / (1.0 + tail) * (share * share)
-    per_step_ref[...] = slope / jnp.where(dt > 0.0, dt, 1.0)
-    per_sum_ref[...] = slope * x_ref[...].astype(F32)
+    slope_ref[...] = jnp.where(pre >= 0.0, 1.0, tail) / (1.0 + tail) * (share * share)
     put(dt_scr, dt)
     put(dtx_scr, dt * x_ref[...].astype(F32))
 
@@ -133,7 +131,7 @@
             last_ref[pl.ds(k * SUB, SUB), sl(g)] = hn[g][k]
 
 
-def scan_fwd(low_t, wdt, bias, x, bt, ct, alog, span=LANES, width=1024):
+def scan_fwd(low_t, wdt, bias, x, bt, ct, alog, span=LANES, width=512):
     count, channels = x.shape
     width = min(width, channels)
     nt, nb, rank = count // span, channels // width, wdt.shape[0]
@@ -158,14 +156,12 @@
             tile,
             tile,
             tile,
-            tile,
             pl.BlockSpec((span * STATE, width), lambda t, c: (t, c)),
             pl.BlockSpec((STATE, width), lambda t, c: (0, c)),
             lanes,
             lanes,
         ],
         out_shape=[
-            jax.ShapeDtypeStruct((count, channels), F32),
             jax.ShapeDtypeStruct((count, channels), F32),
             jax.ShapeDtypeStruct((count, channels), F32),
             jax.ShapeDtypeStruct((count, channels), F32),
@@ -180,12 +176,12 @@
             pltpu.VMEM((groups, span, LANES), F32),
             pltpu.VMEM((groups, SUB * SUB, LANES), F32),
         ],
-        compiler_params=pltpu.CompilerParams(vmem_limit_bytes=58 << 20),
+        compiler_params=pltpu.CompilerParams(vmem_limit_bytes=48 << 20),
         cost_estimate=work(60e-6),
     )(low_t, wdt, bias.reshape(1, -1), x, bt, ct, alog)
 
 
-def bwd_kernel(lowt_ref, wdt_ref, x_ref, dm_ref, dt_ref, per_step_ref, per_sum_ref, hs_ref, last_ref, bl_ref, cl_ref, alog_ref, dskip_ref,
+def bwd_kernel(lowt_ref, wdt_ref, x_ref, dm_ref, dt_ref, slope_ref, hs_ref, last_ref, bl_ref, cl_ref, alog_ref, dskip_ref,
                dx_ref, dcp_ref, gwdt_ref, gal_ref, gvec_ref,
                part_scr, g_scr, n_scr, dt_scr, dtx_scr, dm_scr, p1_scr, p2_scr, s1_scr, s2_scr, db_scr, dc_scr):
     span, width = x_ref.shape
@@ -272,7 +268,7 @@
     s1 = take(s1_scr)
     s2 = take(s2_scr) * (1.0 / LOG2E)
     dx_ref[...] = dm * dskip_ref[...] + dt * s1
-    d_pre = s2 * per_step_ref[...] + s1 * per_sum_ref[...]
+    d_pre = (s2 / jnp.where(dt > 0.0, dt, 1.0) + x * s1) * slope_ref[...]
     gvec_ref[cb, 0:1, :] += jnp.sum(d_pre, axis=0, keepdims=True)
     gvec_ref[cb, 1:2, :] += jnp.sum(dm * x, axis=0, keepdims=True)
     dlow = d_pre.astype(BF)
@@ -296,7 +292,7 @@
             dcp_ref[at : at + STATE, :] = jnp.dot(kept, pick, preferred_element_type=F32).astype(dcp_ref.dtype)
 
 
-def scan_bwd(low_t, wdt, x, dm, dt, per_step, per_sum, hs, last, bl, cl, alog, dskip, span=LANES, width=1024):
+def scan_bwd(low_t, wdt, x, dm, dt, slope, hs, last, bl, cl, alog, dskip, span=LANES, width=512):
     count, channels = x.shape
     width = min(width, channels)
     nt, nb, rank = count // span, channels // width, wdt.shape[0]
@@ -314,7 +310,6 @@
             tile,
             tile,
             tile,
-            tile,
             pl.BlockSpec((span * STATE, width), lambda t, c: (nt - 1 - t, c)),
             pl.BlockSpec((STATE, width), lambda t, c: (0, c)),
             lanes,
@@ -344,9 +339,9 @@
             *[pltpu.VMEM((groups, span, LANES), F32)] * 2,
             *[pltpu.VMEM((span * STATE, LANES), F32)] * 2,
         ],
-        compiler_params=pltpu.CompilerParams(vmem_limit_bytes=58 << 20),
+        compiler_params=pltpu.CompilerParams(vmem_limit_bytes=48 << 20),
         cost_estimate=work(110e-6),
-    )(low_t, wdt, x, dm, dt, per_step, per_sum, hs, last, bl, cl, alog, dskip.reshape(1, -1))
+    )(low_t, wdt, x, dm, dt, slope, hs, last, bl, cl, alog, dskip.reshape(1, -1))
 
 
 def taps_at(pad_ref, g, row, rows):
@@ -648,8 +643,8 @@
     cot_own = after(cotangent[0], normed)
     cot_other = swap(cot_own) if paired_tensor else lax.all_gather(cot_own, "tensor", axis=0, tiled=True)
     w_inner = lax.all_gather(w_in[:, 0], "dp", axis=0, tiled=True)
-    w_gate = lax.all_gather(after(w_in, scale)[:, 1], "dp", axis=0, tiled=True)
-    out_full = lax.all_gather(after(w_out, scale).T, "dp", axis=0, tiled=True)
+    w_gate = lax.all_gather(w_in[:, 1], "dp", axis=0, tiled=True)
+    out_full = lax.all_gather(w_out, "dp", axis=1, tiled=True)
     w_x_t = w_x.T
 
     inner = mm(normed, w_inner)
@@ -663,7 +658,7 @@
     else:
         coupled = total_tensor(part)
     low_t = coupled[:RANK].astype(BF)
-    scanned, step_size, per_step, per_sum, states, last, input_lanes, output_lanes = scan_fwd(
+    scanned, step_size, slope, states, last, input_lanes, output_lanes = scan_fwd(
         low_t, w_dt, dt_bias, conv_low, coupled[RANK : RANK + STATE], coupled[RANK + STATE :], a_log
     )
     w_gate, scanned = lax.optimization_barrier((w_gate, scanned))
@@ -679,7 +674,7 @@
     part_out = mm_tn(d_branch, gated).astype(BF)
     g_w_out = spread(part_out)
     out_full = after(out_full, part_out)
-    d_gated = mm(d_branch, out_full)
+    d_gated = mm_nt(d_branch, out_full)
     d_mixed = d_gated * opened
     d_gate = (d_gated * mixed * (sig * (1.0 + gate_in * (1.0 - sig)))).astype(BF)
     part_gate = mm_tn(normed, d_gate).astype(BF)
@@ -690,7 +685,7 @@
 
     d_mixed = after(d_mixed, part_gate)
     if not paired_tensor:
-        branch = lax.psum_scatter(mm_nt(gated, out_full), "tensor", scatter_dimension=0, tiled=True)
+        branch = lax.psum_scatter(mm(gated, out_full), "tensor", scatter_dimension=0, tiled=True)
 
     d_scan, d_part, g_w_dt, g_a_log, g_vec = scan_bwd(
         low_t,
@@ -698,8 +693,7 @@
         conv_low,
         d_mixed,
         step_size,
-        per_step,
-        per_sum,
+        slope,
         states,
         last,
         input_lanes,
@@ -717,7 +711,7 @@
         return jnp.concatenate([p.astype(BF) for p in pieces] + [jnp.zeros((padded - held, width), BF)], axis=0)
 
     if paired_tensor:
-        branch_sent = mm_nt(after(halves(gated, 1 - side), d_part), out_full).astype(BF)
+        branch_sent = mm(after(halves(gated, 1 - side), d_part), out_full).astype(BF)
         d_coupled = (d_part.astype(F32) + after(swap(d_part), branch_sent).astype(F32)).astype(BF)
         branch_got = swap(after(branch_sent, d_coupled))
     else:
@@ -732,7 +726,7 @@
         )
         g_gain = lax.psum(jnp.sum(residual * scale * d_normed, axis=0), ("dp", "tensor"))
         if paired_tensor:
-            branch = mm_nt(halves(gated, side), out_full) + branch_got.astype(F32)
+            branch = mm(halves(gated, side), out_full) + branch_got.astype(F32)
         d_rows = rows_back(cotangent, residual, scale, gain, d_normed)
         mixed_out = rows_out(residual, branch, length, side * rows_here)
     else:
@@ -770,7 +764,7 @@
         x_got = over_x(whole)
         g_gain = g_gain + after(gain_got, whole)
         gain_got = over_x(g_gain)
-        branch = mm_nt(after(halves(gated, side), g_gain), out_full) + branch_got.astype(F32)
+        branch = mm(after(halves(gated, side), g_gain), out_full) + branch_got.astype(F32)
         mixed_out = rows_out(residual, branch, length, side * rows_here)
         half = paired(whole, after(x_got, mixed_out), x)
         core_got = over_core(half)

time: 772 us -> 768 us (level)
    dot_general x2 -> x1, matrix products: 15.8 us -> 23.1 us  [mm_nt(): lax.dot_general(a, b, (((1,), (1,)), ((), ())), preferred_element_type=F32)]
    dot_general x3 -> x4, matrix products: 53.2 us -> 46.5 us  [mm(): return jnp.dot(a, b, preferred_element_type=F32)]
    unnamed x85 -> x82, local copies, waits for them, and re-layouts: 16.8 us -> 17 us
  transfers between devices with their start and end apart: 28 -> 28, of which waited for: 11 -> 11; matrix products, arithmetic and copies ran while one was open for 15% -> 14% of each run, Pallas kernels for 14% -> 14%
where the time goes in v1:
time: 768 us; the launch traced here: 765 us
  waiting for transfers between devices  296 us (39%)
  Pallas kernels  243 us (32%)
  matrix products  113 us (15%)
  other arithmetic  35.4 us (5%)
  starting transfers between devices  31.8 us (4%)
  local copies, waits for them, and re-layouts  30.3 us (4%)
  between operations  15.9 us (2%)
    reduce_scatter x3, waiting for transfers between devices, spread(): return lax.psum_scatter(grad, 'dp', scatter_dimension=0, tiled=True)  191 us
    pallas_call x1, Pallas kernels, scan_bwd(): pl.pallas_call(bwd_kernel, name='scan_bwd', grid=(nt, nb), in_specs=[pl.B...  111 us
    pallas_call x1, Pallas kernels, scan_fwd(): pl.pallas_call(fwd_kernel, name='scan_fwd', grid=(nt, nb), in_specs=[pl.B...  76.9 us
    ppermute x7, waiting for transfers between devices, swap(): return lax.ppermute(value, 'tensor', [(0, 1), (1, 0)])  54.7 us
    dot_general x4, matrix products, mm(): return jnp.dot(a, b, preferred_element_type=F32)  46.5 us
    dot_general x4, matrix products, mm_tn(): lax.dot_general(a, b, (((0,), (0,)), ((), ())), preferred_element_type=F32)  43 us
    pallas_call x2, Pallas kernels, dual_product(): pl.pallas_call(dual_kernel, name='dual_product', grid_spec=pltpu.Prefetch...  24.5 us
    dot_general x1, matrix products, mm_nt(): lax.dot_general(a, b, (((1,), (1,)), ((), ())), preferred_element_type=F32)  23.1 us
  transfers between devices with their start and end apart: 28, of which 11 were waited for; matrix products, arithmetic and copies ran while one was open for 14% of the time, Pallas kernels for 14%

profile of v1, /device:TPU:0, one launch (start us, length us, event | category | flops | bytes accessed | tf_op | source)
XLA Modules:
  0.0 764.8 jit_solution(8210554570851177354)
XLA Ops:
  7.2 3.3 fusion.19
  10.6 1.1 copy.42
  11.8 1.1 copy.41
  14.0 1.9 fusion.4
  15.9 3.0 collective-permute-start
  19.8 45.0 %collective-permute-done = bf16[512,2048]{1,0:T(8,128)(2,1)} collective-permute-done((bf16[512,2048]{1,0:T(8,128)(2,1)}, bf16[512,2048]{1,0:T(8,128)(2,1)}, u32[]{:S(2)}, u32[]{:S(2)}) %collective-permute-start) | collective-permute-done | bytes 2097184 | tf_op jit(solution)/shard_map/ppermute | solution.py:529
  64.8 3.1 broadcast_select_fusion.3
  67.9 2.6 pad_maximum_fusion.norm_ref
  71.4 1.8 collective-permute-start.1
  73.2 15.7 %all-gather.10.cloned.1.call-done = bf16[2048,1,2048]{2,0,1:T(8,128)(2,1)} async-done(((bf16[128,1,2048]{2,0,1:T(8,128)(2,1)}), bf16[2048,1,2048]{2,0,1:T(8,128)(2,1)}) %all-gather.10.cloned.1.call-update) | async-done | bytes 8388624 | tf_op jit(solution)/shard_map/all_gather | solution.py:645
  88.9 12.5 %fusion.15.inner_ref = f32[1024,2048]{1,0:T(8,128)S(1)} fusion(bf16[2048,1,2048]{2,0,1:T(8,128)(2,1)} %all-gather.10.cloned.1.call-done, bf16[512,2048]{1,0:T(8,128)(2,1)} %copy-done.24, bf16[512,2048]{1,0:T(8,128)(2,1)} %copy-done.22), kind=kOutput, calls=%fused_computation.73 | convolution fusion | flops 8598323200 | bytes 20971520 | tf_op jit(solution)/shard_map/dot_general | solution.py:593
  101.4 9.3 %conv_forward.1 = (bf16[1024,2048]{1,0:T(8,128)(2,1)S(1)}, bf16[160,1024]{1,0:T(8,128)(2,1)S(1)}) custom-call(f32[1024,2048]{1,0:T(8,128)S(1)} %fusion.15.inner_ref, bf16[160,2048]{1,0:T(8,128)(2,1)S(1)} %bitcast.89, f32[4,2048]{1,0:T(4,128)S(1)} %copy-done.6, f32[1,2048]{1,0:T(1,128)S(1)} %bitcast.93), custom_call_target="tpu_custom_call" | custom-call | flops 12000000000 | bytes 12000000 | tf_op jit(solution)/shard_map/conv_forward/pallas_call | solution.py:391
  110.8 1.5 collective-permute-start.2
  112.3 7.7 %collective-permute-done.1 = bf16[512,2048]{1,0:T(8,128)(2,1)} collective-permute-done((bf16[512,2048]{1,0:T(8,128)(2,1)S(1)}, bf16[512,2048]{1,0:T(8,128)(2,1)}, u32[]{:S(2)}, u32[]{:S(2)}) %collective-permute-start.1) | collective-permute-done | bytes 2097184 | tf_op jit(solution)/shard_map/ppermute | solution.py:529
  120.0 1.9 broadcast_select_fusion.1
  122.0 7.0 maximum_select_fusion
  129.1 76.9 %scan_fwd.1 = (f32[1024,2048]{1,0:T(8,128)}, f32[1024,2048]{1,0:T(8,128)}, f32[1024,2048]{1,0:T(8,128)}, f32[16384,2048]{1,0:T(8,128)}, f32[16,2048]{1,0:T(8,128...) custom-call(bf16[128,1024]{1,0:T(8,128)(2,1)S(1)} %slice.73.lowt_ref, bf16[128,2048]{1,0:T(8,128)(2,1)S(1)} %copy-done.4, ...), custom_call_target="tpu_custom_call" | custom-call | flops 60000002048 | bytes 60000000 | tf_op jit(solution)/shard_map/scan_fwd/pallas_call | solution.py:142
  206.1 18.4 %multiply_convert_fusion.1 = (bf16[1024,2048]{1,0:T(8,128)(2,1)S(1)}, f32[1024,2048]{1,0:T(8,128)}) fusion(f32[1024,2048]{1,0:T(8,128)} %get-tuple-element.79, bf16[1024,2048]{1,0:T(8,128)(2,1)} %copy-done.16, f32[2048]{0:T(1024)S(1)} %copy-done.9, bf16[2048,2048]{1,0:T(8,128)(2,1)} %bitcast.111, bf16[512,2048]{1,0:T(8,128)(2,1)} %copy-done.24, ...), kind=kOutput, calls=%fused_computation.6 | convolution fusion | flops 8617197568 | bytes 37756928 | tf_op jit(solution)/shard_map/dot_general | solution.py:593
  224.5 2.0 copy-done.27
  226.6 13.6 %convolution_convert_fusion.2 = bf16[2048,2048]{1,0:T(8,128)(2,1)} fusion(bf16[1024,2048]{1,0:T(8,128)(2,1)} %maximum_select_fusion, bf16[1024,2048]{1,0:T(8,128)(2,1)S(1)} %get-tuple-element.178), kind=kOutput, calls=%fused_computation.12 | convolution fusion | flops 8594128896 | bytes 16777216 | tf_op jit(solution)/shard_map/dot_general | solution.py:601
  240.2 3.0 all-gather.6.cloned.1.call-done
  243.1 23.1 %multiply_convert_fusion = (bf16[1024,2048]{1,0:T(8,128)(2,1)}, f32[1024,2048]{1,0:T(8,128)}) fusion(f32[1024,2048]{1,0:T(8,128)} %get-tuple-element.179, f32[1024,2048]{1,0:T(8,128)} %get-tuple-element.79, bf16[1024,2048]{1,0:T(8,128)(2,1)} %copy-done.16, f32[2048]{0:T(1024)S(1)} %copy-done.9, bf16[1024,2048]{1,0:T(8,128)(2,1)} %maximum_select_fusion, ...), kind=kOutput, calls=%fused_computation.5 | convolution fusion | flops 8621391872 | bytes 46145536 | tf_op jit(solution)/shard_map/dot_general | solution.py:597
  266.2 13.7 %convolution_convert_fusion.1 = bf16[2048,2048]{1,0:T(8,128)(2,1)} fusion(bf16[1024,2048]{1,0:T(8,128)(2,1)} %get-tuple-element.154.b_ref, bf16[512,2048]{1,0:T(8,128)(2,1)} %copy-done.24, bf16[512,2048]{1,0:T(8,128)(2,1)S(1)} %copy-done.23), kind=kOutput, calls=%fused_computation.11 | convolution fusion | flops 8602517504 | bytes 16777216 | tf_op jit(solution)/shard_map/dot_general | solution.py:601
  279.9 111.5 %scan_bwd.1 = (f32[1024,2048]{1,0:T(8,128)}, bf16[160,1024]{1,0:T(8,128)(2,1)S(1)}, f32[4,128,512]{2,1,0:T(8,128)S(1)}, f32[4,16,512]{2,1,0:T(8,128)S(1)}, f32[4,2,512]{2,1,0:T(2,128)S(1)}) custom-call(bf16[128,1024]{1,0:T(8,128)(2,1)S(1)} %slice.73.lowt_ref, bf16[128,2048]{1,0:T(8,128)(2,1)S(1)} %copy-done.4, bf16[1024,2048]{1,0:T(8,128)(2,1)} %copy-done.16, ...), custom_call_target="tpu_custom_call" | custom-call | flops 109999996928 | bytes 110000000 | tf_op jit(solution)/shard_map/scan_bwd/pallas_call | solution.py:302
  391.4 1.5 collective-permute-start.3
  392.9 1.6 constant_dynamic-slice_fusion.2
  394.6 1.0 copy-done.38
  395.6 5.9 convolution_convert_fusion.4
  402.5 21.1 %conv_back.1 = (bf16[1024,2048]{1,0:T(8,128)(2,1)S(1)}, f32[8,2048]{1,0:T(8,128)S(1)}, f32[160,2048]{1,0:T(8,128)S(1)}) custom-call(f32[1024,2048]{1,0:T(8,128)} %copy-done.14, f32[1024,2048]{1,0:T(8,128)} %get-tuple-element.89.dx_ref, bf16[1024,160]{1,0:T(8,128)(2,1)S(1)} %copy.34.dcp_ref, bf16[160,1024]{1,0:T(8,128)(2,1)S(1)} %add_convert_fusion.4.dcpt_ref, ...), custom_call_target="tpu_custom_call" | custom-call | flops 15000000512 | bytes 15000000 | tf_op jit(solution)/shard_map/conv_back/pallas_call | solution.py:463
  423.7 2.0 copy-done.12
  425.8 1.1 concatenate.20
  427.2 8.2 %convolution_convert_fusion = bf16[2048,1152]{1,0:T(8,128)(2,1)S(1)} fusion(bf16[1024,2048]{1,0:T(8,128)(2,1)} %pad_maximum_fusion.norm_ref, bf16[1024,2048]{1,0:T(8,128)(2,1)} %copy-done.12), kind=kOutput, calls=%fused_computation.10 | convolution fusion | flops 4834197504 | bytes 11272192 | tf_op jit(solution)/shard_map/dot_general | solution.py:601
  435.7 2.2 copy-done.25
  437.8 1.6 dynamic-slice_bitcast_fusion
  440.2 7.5 convolution_convert_fusion.3
  448.7 1.5 collective-permute-start.6
  450.3 1.5 collective-permute-start.11
  451.8 6.8 collective-permute-done.6
  458.8 3.3 fusion.1
  462.3 1.6 collective-permute-start.10
  464.2 12.3 %dual_product.2 = (bf16[512,2048]{1,0:T(8,128)(2,1)S(1)}, f32[1,2048]{1,0:T(1,128)S(1)}) custom-call(s32[1]{0:T(128)} %bitcast.9.which_ref, bf16[1024,2048]{1,0:T(8,128)(2,1)S(1)} %copy-done.13, bf16[1024,2048]{1,0:T(8,128)(2,1)S(1)} %copy-done.15, bf16[2048,2048]{1,0:T(8,128)(2,1)} %bitcast.109, bf16[2048,2048]{1,0:T(8,128)(2,1)} %bitcast.112, ...), custom_call_target="tpu_custom_call" | custom-call | flops 15000000512 | bytes 15000000 | tf_op jit(solution)/shard_map/dual_product/pallas_call | solution.py:510
  476.6 1.7 collective-permute-start.9
  478.3 1.5 collective-permute-start.12
  479.8 12.1 %dual_product.3 = (f32[512,2048]{1,0:T(8,128)S(1)}, f32[1,2048]{1,0:T(1,128)S(1)}) custom-call(s32[1]{0:T(128)} %bitcast.21.which_ref, bf16[1024,2048]{1,0:T(8,128)(2,1)S(1)} %copy-done.13, bf16[1024,2048]{1,0:T(8,128)(2,1)S(1)} %copy-done.15, bf16[2048,2048]{1,0:T(8,128)(2,1)} %bitcast.110, bf16[2048,2048]{1,0:T(8,128)(2,1)} %bitcast.113, ...), custom_call_target="tpu_custom_call" | custom-call | flops 15000000512 | bytes 15000000 | tf_op jit(solution)/shard_map/dual_product/pallas_call | solution.py:510
  492.1 7.4 collective-permute-done.10
  500.8 3.6 collective-permute-start.15
  504.4 9.7 %fusion.5 = bf16[512,2048]{1,0:T(8,128)(2,1)} fusion(bf16[512,2048]{1,0:T(8,128)(2,1)S(1)} %collective-permute-done.11, bf16[1,512,2048]{2,1,0:T(8,128)(2,1)S(1)} %copy-done.18, pred[512]{0:T(512)(128)(4,1)S(1)} %add_compare_fusion, bf16[512,2048]{1,0:T(8,128)(2,1)S(1)} %copy-done.31, bf16[2048,2048]{1,0:T(8,128)(2,1)} %all-gather.6.cloned.1.call-done), kind=kOutput, calls=%fused_computation.18 | convolution fusion | flops 4301258752 | bytes 16777728 | tf_op jit(solution)/shard_map/dot_general | solution.py:593
  516.6 2.5 collective-permute-start.20
  519.5 2.6 collective-permute-start.21
  522.1 1.6 broadcast_select_fusion.5
  524.0 16.2 %collective-permute-done.14 = f32[1,2048]{1,0:T(1,128)S(1)} collective-permute-done((f32[1,2048]{1,0:T(1,128)S(1)}, f32[1,2048]{1,0:T(1,128)S(1)}, u32[]{:S(2)}, u32[]{:S(2)}) %collective-permute-start.14) | collective-permute-done | bytes 8224 | tf_op jit(solution)/shard_map/ppermute | solution.py:563
  540.3 4.0 collective-permute-start.17
  544.4 2.6 fusion.8
  547.0 1.2 slice_bitcast_fusion
  548.2 4.7 fusion.7
  553.5 1.1 slice.63
  555.9 1.5 collective-permute-start.18
  557.6 2.0 collective-permute-done.18
  560.2 1.0 convert_element_type.239
  561.3 83.6 %reduce-scatter.6.cloned.1.call-done = bf16[128,2048]{1,0:T(8,128)(2,1)} async-done(((bf16[2048,2048]{1,0:T(8,128)(2,1)}), bf16[128,2048]{1,0:T(8,128)(2,1)}) %reduce-scatter.6.cloned.1.call-update) | async-done | bytes 524304 | tf_op jit(solution)/shard_map/reduce_scatter | solution.py:672
  644.9 107.0 %reduce-scatter.8.cloned.1.call-done = bf16[128,2048]{1,0:T(8,128)(2,1)} async-done(((bf16[2048,2048]{1,0:T(8,128)(2,1)}), bf16[128,2048]{1,0:T(8,128)(2,1)}) %reduce-scatter.8.cloned.1.call-update) | async-done | bytes 524304 | tf_op jit(solution)/shard_map/reduce_scatter | solution.py:672
  751.9 1.1 bitcast_convert_fusion
  753.3 2.9 copy.39
  756.4 1.3 copy.40
  (156 shorter events, 14.5 us)
Async XLA Ops:
  7.2 5.8 copy-start.17
  7.2 81.7 %all-gather.10.cloned.1.call-start = ((), (), s32[]{:S(2)}) async-start(), calls=%async_computation.8 | async-start | bytes 8912896 | tf_op jit(solution)/shard_map/all_gather | solution.py:645
  10.6 3.4 copy-start.33
  11.7 194.4 %all-gather.8.cloned.1.call-start = ((), (), s32[]{:S(2)}) async-start(), calls=%async_computation.7 | async-start | bytes 8912896 | tf_op jit(solution)/shard_map/all_gather | solution.py:646
  12.9 230.3 %all-gather.6.cloned.1.call-start = ((), (), s32[]{:S(2)}) async-start(), calls=%async_computation.3 | async-start | bytes 8912896 | tf_op jit(solution)/shard_map/all_gather | solution.py:647
  14.0 53.9 %copy-start.35 = (f32[512]{0:T(512)}, f32[512]{0:T(512)S(1)}, u32[]{:S(2)}) copy-start(f32[512]{0:T(512)S(1)} %get-tuple-element.177) | copy-start | bytes 6148
  15.9 48.9 %collective-permute-start = (bf16[512,2048]{1,0:T(8,128)(2,1)}, bf16[512,2048]{1,0:T(8,128)(2,1)}, u32[]{:S(2)}, u32[]{:S(2)}) collective-permute-start(bf16[512,2048]{1,0:T(8,128)(2,1)} %fusion.4), channel_id=1, source_target_pairs={{0,1},{1,0},{2,3},{3,2},{4,5},{5,4},{6,7},{7,6},{8,9},{9,8},{10,11... | collective-permute-start | bytes 6291464 | tf_op jit(solution)/shard_map/ppermute | solution.py:529
  18.9 541.3 %reduce-scatter.4.cloned.1.call-start = ((), (), s32[]{:S(2)}) async-start(), calls=%async_computation.4 | async-start | bytes 3899392 | tf_op jit(solution)/shard_map/reduce_scatter | solution.py:672
  67.9 2.8 copy-start.22
  67.9 3.4 copy-start.24
  67.9 3.4 copy-start.20
  71.4 30.0 %copy-start.2 = (bf16[2048,160]{0,1:T(8,128)(2,1)S(1)}, bf16[2048,160]{0,1:T(8,128)(2,1)}, u32[]{:S(2)}) copy-start(bf16[2048,160]{0,1:T(8,128)(2,1)} %param.19) | copy-start | bytes 1966084
  71.4 30.0 %copy-start.6 = (f32[4,2048]{1,0:T(4,128)S(1)}, f32[4,2048]{1,0:T(4,128)}, u32[]{:S(2)}) copy-start(f32[4,2048]{1,0:T(4,128)} %cw_ref.3) | copy-start | bytes 98308
  71.4 30.0 %copy-start.10 = (f32[2048]{0:T(1024)S(1)}, f32[2048]{0:T(1024)}, u32[]{:S(2)}) copy-start(f32[2048]{0:T(1024)} %param.18) | copy-start | bytes 24580
  71.4 48.7 %collective-permute-start.1 = (bf16[512,2048]{1,0:T(8,128)(2,1)S(1)}, bf16[512,2048]{1,0:T(8,128)(2,1)}, u32[]{:S(2)}, u32[]{:S(2)}) collective-permute-start(bf16[512,2048]{1,0:T(8,128)(2,1)S(1)} %bitcast.97), channel_id=1, source_target_pairs={{0,1},{1,0},{2,3},{3,2},{4,5},{5,4},{6,7},{7,6},{8,9},{9,8},{10,11... | collective-permute-start | bytes 6291464 | tf_op jit(solution)/shard_map/ppermute | solution.py:529
  101.4 9.4 %copy-start.14 = (f32[1024,2048]{1,0:T(8,128)}, f32[1024,2048]{1,0:T(8,128)S(1)}, u32[]{:S(2)}) copy-start(f32[1024,2048]{1,0:T(8,128)S(1)} %fusion.15.inner_ref) | copy-start | bytes 25165828
  110.8 18.3 %copy-start.16 = (bf16[1024,2048]{1,0:T(8,128)(2,1)}, bf16[1024,2048]{1,0:T(8,128)(2,1)S(1)}, u32[]{:S(2)}) copy-start(bf16[1024,2048]{1,0:T(8,128)(2,1)S(1)} %get-tuple-element.77.x_ref) | copy-start | bytes 12582916
  110.8 18.1 %collective-permute-start.2 = (bf16[160,1024]{1,0:T(8,128)(2,1)S(1)}, bf16[160,1024]{1,0:T(8,128)(2,1)S(1)}, u32[]{:S(2)}, u32[]{:S(2)}) collective-permute-start(bf16[160,1024]{1,0:T(8,128)(2,1)S(1)} %get-tuple-element.73), channel_id=1, source_target_pairs={{0,1},{1,0},{2,3},{3,2},{4,5},{5,4},{6,7},{7,6},{8,9},{9,8},{10,11... | collective-permute-start | bytes 983048 | tf_op jit(solution)/shard_map/ppermute | solution.py:529
  121.9 7.2 copy-start.4
  121.9 7.2 copy-start.5
  121.9 7.2 copy-start.8
  129.1 77.0 %copy-start.9 = (f32[2048]{0:T(1024)S(1)}, f32[2048]{0:T(1024)}, u32[]{:S(2)}) copy-start(f32[2048]{0:T(1024)} %param.23) | copy-start | bytes 24580
  129.1 77.0 %copy-start.23 = (bf16[512,2048]{1,0:T(8,128)(2,1)S(1)}, bf16[512,2048]{1,0:T(8,128)(2,1)}, u32[]{:S(2)}) copy-start(bf16[512,2048]{1,0:T(8,128)(2,1)} %copy-done.22) | copy-start | bytes 6291460
  224.5 2.0 copy-start.27
  279.9 113.0 %copy-start.28 = (bf16[1024,2048]{1,0:T(8,128)(2,1)S(1)}, bf16[1024,2048]{1,0:T(8,128)(2,1)}, u32[]{:S(2)}) copy-start(bf16[1024,2048]{1,0:T(8,128)(2,1)} %copy-done.27) | copy-start | bytes 12582916
  391.4 4.1 copy-start.38
  391.4 10.2 %collective-permute-start.3 = (bf16[160,1024]{1,0:T(8,128)(2,1)S(1)}, bf16[160,1024]{1,0:T(8,128)(2,1)S(1)}, u32[]{:S(2)}, u32[]{:S(2)}) collective-permute-start(bf16[160,1024]{1,0:T(8,128)(2,1)S(1)} %get-tuple-element.90), channel_id=1, source_target_pairs={{0,1},{1,0},{2,3},{3,2},{4,5},{5,4},{6,7},{7,6},{8,9},{9,8},{10,11... | collective-permute-start | bytes 983048 | tf_op jit(solution)/shard_map/ppermute | solution.py:529
  401.5 1.1 copy-start.11
  423.7 2.0 copy-start.12
  426.9 8.5 %collective-permute-start.4 = (bf16[160,2048]{1,0:T(8,128)(2,1)S(1)}, bf16[160,2048]{1,0:T(8,128)(2,1)S(1)}, u32[]{:S(2)}, u32[]{:S(2)}) collective-permute-start(bf16[160,2048]{1,0:T(8,128)(2,1)S(1)} %constant_dynamic-slice_fusion.1), channel_id=1, source_target_pairs={{0,2},{2,0},{4,6},{6,4},{8,10},{10,8},{12,14},{14,12},{16,18},{18,... | collective-permute-start | bytes 1966088 | tf_op jit(solution)/shard_map/ppermute | solution.py:555
  435.4 2.4 copy-start.25
  435.5 4.7 copy-start.26
  447.7 197.2 %reduce-scatter.6.cloned.1.call-start = ((), (), s32[]{:S(2)}) async-start(), calls=%async_computation.5 | async-start | bytes 8912896 | tf_op jit(solution)/shard_map/reduce_scatter | solution.py:672
  448.3 303.6 %reduce-scatter.8.cloned.1.call-start = ((), (), s32[]{:S(2)}) async-start(), calls=%async_computation.6 | async-start | bytes 8912896 | tf_op jit(solution)/shard_map/reduce_scatter | solution.py:672
  448.4 10.5 %collective-permute-start.5 = (bf16[8,128,1152]{2,1,0:T(8,128)(2,1)}, bf16[8,128,1152]{2,1,0:T(8,128)(2,1)}, u32[]{:S(2)}, u32[]{:S(2)}) collective-permute-start(bf16[8,128,1152]{2,1,0:T(8,128)(2,1)} %dynamic-slice_bitcast_fusion), channel_id=1, source_target_pairs={{0,2},{2,0},{4,6},{6,4},{8,10},{10,8},{12,14},{14,12},{16,18},{18,... | collective-permute-start | bytes 7077896 | tf_op jit(solution)/shard_map/ppermute | solution.py:555
  448.7 9.9 %collective-permute-start.6 = (bf16[80,2048]{1,0:T(8,128)(2,1)S(1)}, bf16[80,2048]{1,0:T(8,128)(2,1)S(1)}, u32[]{:S(2)}, u32[]{:S(2)}) collective-permute-start(bf16[80,2048]{1,0:T(8,128)(2,1)S(1)} %constant_dynamic-slice_fusion), channel_id=1, source_target_pairs={{0,4},{2,6},{4,0},{6,2},{8,12},{10,14},{12,8},{14,10},{16,20},{18,... | collective-permute-start | bytes 983048 | tf_op jit(solution)/shard_map/ppermute | solution.py:559
  450.3 54.1 %collective-permute-start.11 = (bf16[512,2048]{1,0:T(8,128)(2,1)}, bf16[512,2048]{1,0:T(8,128)(2,1)S(1)}, u32[]{:S(2)}, u32[]{:S(2)}) collective-permute-start(bf16[512,2048]{1,0:T(8,128)(2,1)} %convolution_convert_fusion.4), channel_id=1, source_target_pairs={{0,1},{1,0},{2,3},{3,2},{4,5},{5,4},{6,7},{7,6},{8,9},{9,8},{10,11... | collective-permute-start | bytes 6291464 | tf_op jit(solution)/shard_map/ppermute | solution.py:529
  458.7 5.1 copy-start.13
  458.7 5.5 copy-start.15
  458.8 17.8 %collective-permute-start.7 = (bf16[80,2048]{1,0:T(8,128)(2,1)S(1)}, bf16[80,2048]{1,0:T(8,128)(2,1)S(1)}, u32[]{:S(2)}, u32[]{:S(2)}) collective-permute-start(bf16[80,2048]{1,0:T(8,128)(2,1)S(1)} %add_convert_fusion.3), channel_id=1, source_target_pairs={{0,8},{2,10},{4,12},{6,14},{8,0},{10,2},{12,4},{14,6},{16,24},{18,... | collective-permute-start | bytes 983048 | tf_op jit(solution)/shard_map/ppermute | solution.py:563
  462.3 37.2 %collective-permute-start.10 = (bf16[4,128,1152]{2,1,0:T(8,128)(2,1)S(1)}, bf16[4,128,1152]{2,1,0:T(8,128)(2,1)S(1)}, u32[]{:S(2)}, u32[]{:S(2)}) collective-permute-start(bf16[4,128,1152]{2,1,0:T(8,128)(2,1)S(1)} %dynamic-slice_bitcast_fusion.1), channel_id=1, source_target_pairs={{0,4},{2,6},{4,0},{6,2},{8,12},{10,14},{12,8},{14,10},{16,20},{18,... | collective-permute-start | bytes 3538952 | tf_op jit(solution)/shard_map/ppermute | solution.py:559
  476.6 24.1 %collective-permute-start.9 = (bf16[80,2048]{1,0:T(8,128)(2,1)S(1)}, bf16[80,2048]{1,0:T(8,128)(2,1)S(1)}, u32[]{:S(2)}, u32[]{:S(2)}) collective-permute-start(bf16[80,2048]{1,0:T(8,128)(2,1)S(1)} %add_convert_fusion.2), channel_id=1, source_target_pairs={{0,16},{2,18},{4,20},{6,22},{8,24},{10,26},{12,28},{14,30},{16,0},... | collective-permute-start | bytes 983048 | tf_op jit(solution)/shard_map/ppermute | solution.py:567
  478.3 66.0 %collective-permute-start.12 = (bf16[512,2048]{1,0:T(8,128)(2,1)S(1)}, bf16[512,2048]{1,0:T(8,128)(2,1)}, u32[]{:S(2)}, u32[]{:S(2)}) collective-permute-start(bf16[512,2048]{1,0:T(8,128)(2,1)S(1)} %get-tuple-element.107), channel_id=1, source_target_pairs={{0,1},{1,0},{2,3},{3,2},{4,5},{5,4},{6,7},{7,6},{8,9},{9,8},{10,11... | collective-permute-start | bytes 6291464 | tf_op jit(solution)/shard_map/ppermute | solution.py:529
  491.9 22.2 %copy-start = (f32[512,2048]{1,0:T(8,128)}, f32[512,2048]{1,0:T(8,128)S(1)}, u32[]{:S(2)}) copy-start(f32[512,2048]{1,0:T(8,128)S(1)} %get-tuple-element.111) | copy-start | bytes 12582916
  491.9 12.5 %copy-start.18 = (bf16[1,512,2048]{2,1,0:T(8,128)(2,1)S(1)}, bf16[1,512,2048]{2,1,0:T(8,128)(2,1)}, u32[]{:S(2)}) copy-start(bf16[1,512,2048]{2,1,0:T(8,128)(2,1)} %param.13) | copy-start | bytes 6291460
  491.9 12.5 %copy-start.31 = (bf16[512,2048]{1,0:T(8,128)(2,1)S(1)}, bf16[512,2048]{1,0:T(8,128)(2,1)}, u32[]{:S(2)}) copy-start(bf16[512,2048]{1,0:T(8,128)(2,1)} %get-tuple-element.115) | copy-start | bytes 6291460
  492.0 12.4 %collective-permute-start.8 = (f32[1,2048]{1,0:T(1,128)S(1)}, f32[1,2048]{1,0:T(1,128)S(1)}, u32[]{:S(2)}, u32[]{:S(2)}) collective-permute-start(f32[1,2048]{1,0:T(1,128)S(1)} %add.200), channel_id=1, source_target_pairs={{0,2},{2,0},{4,6},{6,4},{8,10},{10,8},{12,14},{14,12},{16,18},{18,... | collective-permute-start | bytes 24584 | tf_op jit(solution)/shard_map/ppermute | solution.py:555
  500.8 13.3 %collective-permute-start.15 = (bf16[80,2048]{1,0:T(8,128)(2,1)S(1)}, bf16[80,2048]{1,0:T(8,128)(2,1)S(1)}, u32[]{:S(2)}, u32[]{:S(2)}) collective-permute-start(bf16[80,2048]{1,0:T(8,128)(2,1)S(1)} %add_convert_fusion.1), channel_id=1, source_target_pairs={{0,4},{2,6},{4,0},{6,2},{8,12},{10,14},{12,8},{14,10},{16,20},{18,... | collective-permute-start | bytes 983048 | tf_op jit(solution)/shard_map/ppermute | solution.py:559
  514.2 1.6 copy-start.30
  514.2 30.1 %copy-start.34 = (f32[2048]{0:T(1024)S(1)}, f32[2048]{0:T(1024)}, u32[]{:S(2)}) copy-start(f32[2048]{0:T(1024)} %param.15) | copy-start | bytes 24580
  515.8 6.2 collective-permute-start.16
  515.8 3.7 collective-permute-start.13
  515.8 28.5 %copy-start.1 = (f32[512,2048]{1,0:T(8,128)S(1)}, f32[512,2048]{1,0:T(8,128)}, u32[]{:S(2)}) copy-start(f32[512,2048]{1,0:T(8,128)} %copy-done) | copy-start | bytes 12582916
  515.9 28.5 %copy-start.19 = (bf16[1,512,2048]{2,1,0:T(8,128)(2,1)S(1)}, bf16[1,512,2048]{2,1,0:T(8,128)(2,1)}, u32[]{:S(2)}) copy-start(bf16[1,512,2048]{2,1,0:T(8,128)(2,1)} %param.13) | copy-start | bytes 6291460
  515.9 41.5 %collective-permute-start.19 = (bf16[128,1152]{1,0:T(8,128)(2,1)}, bf16[128,1152]{1,0:T(8,128)(2,1)S(1)}, u32[]{:S(2)}, u32[]{:S(2)}) collective-permute-start(bf16[128,1152]{1,0:T(8,128)(2,1)} %get-tuple-element.169), channel_id=1, source_target_pairs={{0,8},{2,10},{4,12},{6,14},{8,16},{10,18},{12,20},{14,22},{16,24},... | collective-permute-start | bytes 884744 | tf_op jit(solution)/shard_map/ppermute | solution.py:571
  516.6 40.8 %collective-permute-start.20 = (bf16[128,1152]{1,0:T(8,128)(2,1)}, bf16[128,1152]{1,0:T(8,128)(2,1)S(1)}, u32[]{:S(2)}, u32[]{:S(2)}) collective-permute-start(bf16[128,1152]{1,0:T(8,128)(2,1)} %get-tuple-element.168), channel_id=1, source_target_pairs={{0,16},{2,18},{4,20},{6,22},{8,24},{10,26},{12,28},{14,30},{16,0},... | collective-permute-start | bytes 884744 | tf_op jit(solution)/shard_map/ppermute | solution.py:571
  519.5 37.9 %collective-permute-start.21 = (bf16[128,1152]{1,0:T(8,128)(2,1)}, bf16[128,1152]{1,0:T(8,128)(2,1)S(1)}, u32[]{:S(2)}, u32[]{:S(2)}) collective-permute-start(bf16[128,1152]{1,0:T(8,128)(2,1)} %get-tuple-element.167), channel_id=1, source_target_pairs={{0,24},{2,26},{4,28},{6,30},{8,0},{10,2},{12,4},{14,6},{16,8},{18,... | collective-permute-start | bytes 884744 | tf_op jit(solution)/shard_map/ppermute | solution.py:571
  522.1 18.2 %collective-permute-start.14 = (f32[1,2048]{1,0:T(1,128)S(1)}, f32[1,2048]{1,0:T(1,128)S(1)}, u32[]{:S(2)}, u32[]{:S(2)}) collective-permute-start(f32[1,2048]{1,0:T(1,128)S(1)} %add.216), channel_id=1, source_target_pairs={{0,8},{2,10},{4,12},{6,14},{8,0},{10,2},{12,4},{14,6},{16,24},{18,... | collective-permute-start | bytes 24584 | tf_op jit(solution)/shard_map/ppermute | solution.py:563
  540.3 7.9 %copy-start.21 = (bf16[1,512,2048]{2,1,0:T(8,128)(2,1)S(1)}, bf16[1,512,2048]{2,1,0:T(8,128)(2,1)}, u32[]{:S(2)}) copy-start(bf16[1,512,2048]{2,1,0:T(8,128)(2,1)} %param.25) | copy-start | bytes 6291460
  540.3 7.9 %copy-start.36 = (f32[512]{0:T(512)S(1)}, f32[512]{0:T(512)}, u32[]{:S(2)}) copy-start(f32[512]{0:T(512)} %copy-done.35) | copy-start | bytes 6148
  540.3 7.8 %copy-start.37 = (f32[512]{0:T(512)S(1)}, f32[512]{0:T(512)}, u32[]{:S(2)}) copy-start(f32[512]{0:T(512)} %get-tuple-element.176) | copy-start | bytes 6148
  540.3 15.5 %collective-permute-start.17 = (f32[1,2048]{1,0:T(1,128)S(1)}, f32[1,2048]{1,0:T(1,128)S(1)}, u32[]{:S(2)}, u32[]{:S(2)}) collective-permute-start(f32[1,2048]{1,0:T(1,128)S(1)} %add.217), channel_id=1, source_target_pairs={{0,16},{2,18},{4,20},{6,22},{8,24},{10,26},{12,28},{14,30},{16,0},... | collective-permute-start | bytes 24584 | tf_op jit(solution)/shard_map/ppermute | solution.py:567
  555.9 3.7 collective-permute-start.18
  753.1 3.2 copy-start.32
  (3 other events, 2.9 us)
Sparse Core Ops, SparseCore 0:
  11.8 77.0 all-gather.9
  91.6 72.8 all-gather.7
  166.7 76.4 all-gather.5
  447.8 91.8 reduce-scatter.3
  543.7 101.1 reduce-scatter.5
  648.8 103.0 reduce-scatter.7
